TPU v7x, 32 devices: a whole 2x2x4 slice. The times are simulated.
32 devices in a mesh: gx: 8 (over y, x, core), gy: 4 (over z).
Axes of the slice: x: 2, y: 2, z: 4, core: 2. Of those that a mesh axis runs over, the one named last changes fastest.
Arguments:
- composition: float32 [53, 262144], P(None, ('gx', 'gy')), may hold values from -6 to 6
- particle_mass: float32 [262144], P(('gx', 'gy')), may hold values from 0.3 to 3
- particle_cell: int32 [2, 262144], P(None, ('gx', 'gy')), may hold values from 0 to 511, as said below
- particle_level: int32 [262144], P(('gx', 'gy')), may hold values from 0 to 2, as said below
- les_mean: float32 [53, 32, 512], P(None, 'gx', 'gy'), may hold values from -6 to 6
- mix_rate: float32 [32, 512], P('gx', 'gy'), may hold values from 0.1 to 3
- rate_matrix: float32 [3, 53, 53], replicated, may hold values from -0.875 to 0.875
- implicit_map: float32 [3, 53, 53], replicated, may hold values from -0.875 to 0.875
Outputs:
- updated: float32 [53, 262144], P(None, ('gx', 'gy'))
- cell_means: float32 [53, 32, 512], P(None, 'gx', 'gy')
Inputs may be any that keep to these rules, and one draw needn't show every extreme that they name: `particle_cell`: row 0 is below 32 and row 1 below 512. With the cells split into blocks of 4 x 128 cells in device order (streamwise block index major), every particle's cell lies within 2 cells, in each grid direction, of the block of the device that holds the particle; the distance 2 is reached on every side that has a neighbouring block. `particle_level`: the share of full-mechanism particles differs from device to device, from none to all.
All inputs are finite; a program needn't handle non-finite values.
Results may differ from a plain program's by a relative error of at most 0.0001.
Values sent between devices are 32-bit elements; how exact they have to be, the bound alone decides.
A program may use at most 64 MiB of HBM per device.

v0:
```python
import jax
import jax.numpy as jnp
from jax import lax
from jax.sharding import PartitionSpec as P

NS_LOW = 21
NS_MID = 24
R = 2


prior_weight = 16.0
chem_step = 0.5


def from_behind(value, axis, steps):
    count = lax.axis_size(axis)
    leading, last = (max(0, -steps), min(count, count - steps))
    return lax.ppermute(value, axis, [(source, source + steps) for source in range(leading, last)])


def padded(cells, sides, width):
    for axis, dim in sides:
        count = lax.axis_size(axis)
        ends = count - 1
        head = lax.slice_in_dim(cells, 0, width, axis=dim)
        tail = lax.slice_in_dim(cells, cells.shape[dim] - width, cells.shape[dim], axis=dim)
        cells = jnp.concatenate(
            [
                lax.ppermute(tail, axis, [(i, (i + 1) % count) for i in range(ends)]),
                cells,
                lax.ppermute(head, axis, [((i + 1) % count, i) for i in range(ends)]),
            ],
            axis=dim,
        )
    return cells


def react_padded(mixed_comp, rate_matrix, implicit_map, particle_level):
    species_count = mixed_comp.shape[0]
    species_index = jnp.arange(species_count)
    updated = mixed_comp
    for tier_index, active in enumerate((NS_LOW, NS_MID, species_count)):
        keep_mask = (species_index < active).astype(jnp.float32)[:, None]
        source = keep_mask * jnp.tanh(
            jnp.dot(
                rate_matrix[tier_index],
                keep_mask * mixed_comp,
                precision=lax.Precision.HIGHEST,
                preferred_element_type=jnp.float32,
            )
        )
        change = keep_mask * jnp.dot(
            implicit_map[tier_index],
            source,
            precision=lax.Precision.HIGHEST,
            preferred_element_type=jnp.float32,
        )
        updated = updated + jnp.where(
            particle_level[None, :] == tier_index, chem_step * change, 0.0
        )
    return updated


def rim_slices(field, dim, inner):
    low_rim = lax.slice_in_dim(field, 0, R, axis=dim)
    high_rim = lax.slice_in_dim(field, inner + R, inner + 2 * R, axis=dim)
    return (low_rim, high_rim)


def fold_in(field, dim, inner, from_above, from_below):
    interior = lax.slice_in_dim(field, R, R + inner, axis=dim)
    widths_above = [(0, 0)] * field.ndim
    widths_above[dim] = (inner - R, 0)
    widths_below = [(0, 0)] * field.ndim
    widths_below[dim] = (0, inner - R)
    return interior + jnp.pad(from_above, widths_above) + jnp.pad(from_below, widths_below)


def per_device(
    composition,
    particle_mass,
    particle_cell,
    particle_level,
    les_mean,
    mix_rate,
    rate_matrix,
    implicit_map,
):
    species_count = composition.shape[0]
    block_x = les_mean.shape[1]
    block_y = les_mean.shape[2]
    column_index = lax.axis_index("gx")
    row_index = lax.axis_index("gy")
    cell_x = particle_cell[0]
    cell_y = particle_cell[1]
    span_x = block_x + 2 * R
    span_y = block_y + 2 * R
    local_x = cell_x - (column_index * block_x - R)
    local_y = cell_y - (row_index * block_y - R)
    ext_index = local_x * span_y + local_y
    weighted = composition * particle_mass[None, :]
    ext_sums = (
        jnp.zeros((species_count, span_x * span_y), jnp.float32).at[:, ext_index].add(weighted)
    )
    ext_mass = (
        jnp.zeros((1, span_x * span_y), jnp.float32).at[:, ext_index].add(particle_mass[None, :])
    )
    ext_sums = ext_sums.reshape(species_count, span_x, span_y)
    ext_mass = ext_mass.reshape(1, span_x, span_y)
    low_sums, high_sums = rim_slices(ext_sums, 1, block_x)
    low_mass, high_mass = rim_slices(ext_mass, 1, block_x)
    above_sums, above_mass = from_behind((low_sums, low_mass), "gx", -1)
    below_sums, below_mass = from_behind((high_sums, high_mass), "gx", 1)
    strip_sums = fold_in(ext_sums, 1, block_x, above_sums, below_sums)
    strip_mass = fold_in(ext_mass, 1, block_x, above_mass, below_mass)
    low_sums, high_sums = rim_slices(strip_sums, 2, block_y)
    low_mass, high_mass = rim_slices(strip_mass, 2, block_y)
    above_sums, above_mass = from_behind((low_sums, low_mass), "gy", -1)
    below_sums, below_mass = from_behind((high_sums, high_mass), "gy", 1)
    part_sums = fold_in(strip_sums, 2, block_y, above_sums, below_sums)
    part_mass = fold_in(strip_mass, 2, block_y, above_mass, below_mass)
    cell_means = (part_sums + prior_weight * les_mean) / (part_mass + prior_weight)
    ext_means, ext_rate = (
        padded(cell_means, (("gx", 1), ("gy", 2)), R),
        padded(mix_rate[None], (("gx", 1), ("gy", 2)), R),
    )
    particle_means = jnp.take(ext_means.reshape(species_count, span_x * span_y), ext_index, axis=1)
    particle_rate = jnp.take(ext_rate.reshape(span_x * span_y), ext_index, axis=0)
    factor = 1.0 - jnp.exp(-particle_rate)
    mixed_comp = composition - factor[None, :] * (composition - particle_means)
    updated = react_padded(mixed_comp, rate_matrix, implicit_map, particle_level)
    return (updated, cell_means)


def solution(mesh):
    placed = (
        P(None, ("gx", "gy")),
        P(("gx", "gy")),
        P(None, ("gx", "gy")),
        P(("gx", "gy")),
        P(None, "gx", "gy"),
        P("gx", "gy"),
        P(),
        P(),
    )
    return jax.shard_map(
        per_device,
        mesh=mesh,
        in_specs=placed,
        out_specs=(P(None, ("gx", "gy")), P(None, "gx", "gy")),
        check_vma=False,
    )
```

profile of v0, /device:TPU:1, one launch (start us, length us, event | category | flops | bytes accessed | tf_op | source)
XLA Modules:
  0.0 257.2 jit_solution(15285378805157717824)
XLA Ops:
  1.6 56.9 %scatter_custom_fusion.1 = f32[1056]{0:T(1024)S(1)} fusion(s32[8192]{0:T(1024)S(1)} %bitcast.52, f32[8192]{0:T(1024)} %param.9, f32[]{:T(128)} %constant.36.clone.1), kind=kCustom, calls=%fused_computation.72 | custom fusion | flops 8192 | bytes 4736 | tf_op jit(solution)/shard_map/scatter-add | solution.py:106
  58.6 1.9 collective-permute-start.8
  60.5 4.5 %collective-permute-start.9 = (f32[1,2,132]{2,1,0:T(2,128)S(1)}, f32[1,2,132]{2,1,0:T(2,128)S(1)}, u32[]{:S(2)}, u32[]{:S(2)}) collective-permute-start(f32[1,2,132]{2,1,0:T(2,128)S(1)} %get-tuple-element.16), channel_id=1, source_target_pairs={{0,4},{4,8},{8,12},{12,16},{16,20},{20,24},{24,28},{1,5},{5,9},{9,... | collective-permute-start | bytes 3176 | tf_op jit(solution)/shard_map/ppermute | solution.py:18
  65.0 1.6 multiply_bitcast_fusion
  66.7 2.8 %copy.16 = f32[8192,53]{1,0:T(8,128)} copy(f32[8192,53]{0,1:T(8,128)S(1)} %multiply_bitcast_fusion) | data formatting | bytes 3473408 | tf_op jit(solution)/shard_map/mul | solution.py:101
  69.4 44.5 %scatter_custom_fusion = f32[53,1056]{0,1:T(8,128)S(1)} fusion(s32[8192]{0:T(1024)S(1)} %bitcast.53, f32[8192,53]{1,0:T(8,128)} %copy.16, f32[]{:T(128)} %constant.36.clone.1), kind=kCustom, calls=%fused_computation.36 | custom fusion | flops 434176 | bytes 224384 | tf_op jit(solution)/shard_map/scatter-add | solution.py:103
  114.5 1.9 collective-permute-start.4
  116.5 3.6 %collective-permute-start = (f32[1,2,128]{2,1,0:T(2,128)S(1)}, f32[1,2,128]{2,1,0:T(2,128)S(1)}, u32[]{:S(2)}, u32[]{:S(2)}) collective-permute-start(f32[1,2,128]{2,1,0:T(2,128)S(1)} %get-tuple-element.21), channel_id=1, source_target_pairs={{0,4},{4,8},{8,12},{12,16},{16,20},{20,24},{24,28},{1,5},{5,9},{9,... | collective-permute-start | bytes 3080 | tf_op jit(solution)/shard_map/ppermute | solution.py:29
  120.1 1.9 collective-permute-start.1
  122.2 3.6 %collective-permute-start.5 = (f32[53,2,132]{2,1,0:T(2,128)S(1)}, f32[53,2,132]{2,1,0:T(2,128)S(1)}, u32[]{:S(2)}, u32[]{:S(2)}) collective-permute-start(f32[53,2,132]{2,1,0:T(2,128)S(1)} %get-tuple-element.5), channel_id=1, source_target_pairs={{0,4},{4,8},{8,12},{12,16},{16,20},{20,24},{24,28},{1,5},{5,9},{9,... | collective-permute-start | bytes 167912 | tf_op jit(solution)/shard_map/ppermute | solution.py:18
  125.9 3.2 %collective-permute-start.2 = (f32[1,8,2]{2,1,0:T(8,128)S(1)}, f32[1,8,2]{2,1,0:T(8,128)S(1)}, u32[]{:S(2)}, u32[]{:S(2)}) collective-permute-start(f32[1,8,2]{2,1,0:T(8,128)S(1)} %get-tuple-element.17), channel_id=1, source_target_pairs={{0,1},{1,2},{2,3},{4,5},{5,6},{6,7},{8,9},{9,10},{10,11},{12,13},{... | collective-permute-start | bytes 200 | tf_op jit(solution)/shard_map/ppermute | solution.py:29
  129.1 1.3 collective-permute-start.3
  131.8 4.6 %collective-permute-start.11 = (f32[1,4,2]{2,1,0:T(4,128)S(1)}, f32[1,4,2]{2,1,0:T(4,128)S(1)}, u32[]{:S(2)}, u32[]{:S(2)}) collective-permute-start(f32[1,4,2]{2,1,0:T(4,128)S(1)} %get-tuple-element.20), channel_id=1, source_target_pairs={{0,1},{1,2},{2,3},{4,5},{5,6},{6,7},{8,9},{9,10},{10,11},{12,13},{... | collective-permute-start | bytes 104 | tf_op jit(solution)/shard_map/ppermute | solution.py:18
  136.7 1.3 collective-permute-start.6
  138.1 4.0 %collective-permute-start.7 = (f32[53,4,2]{2,1,0:T(4,128)S(1)}, f32[53,4,2]{2,1,0:T(4,128)S(1)}, u32[]{:S(2)}, u32[]{:S(2)}) collective-permute-start(f32[53,4,2]{2,1,0:T(4,128)S(1)} %get-tuple-element.9), channel_id=1, source_target_pairs={{0,1},{1,2},{2,3},{4,5},{5,6},{6,7},{8,9},{9,10},{10,11},{12,13},{... | collective-permute-start | bytes 5096 | tf_op jit(solution)/shard_map/ppermute | solution.py:18
  142.1 1.4 collective-permute-done.6
  144.8 5.3 %collective-permute-start.12 = (f32[53,2,128]{2,1,0:T(2,128)S(1)}, f32[53,2,128]{2,1,0:T(2,128)S(1)}, u32[]{:S(2)}, u32[]{:S(2)}) collective-permute-start(f32[53,2,128]{2,1,0:T(2,128)S(1)} %get-tuple-element.10), channel_id=1, source_target_pairs={{0,4},{4,8},{8,12},{12,16},{16,20},{20,24},{24,28},{1,5},{5,9},{9,... | collective-permute-start | bytes 162824 | tf_op jit(solution)/shard_map/ppermute | solution.py:29
  150.1 1.9 collective-permute-start.13
  152.2 45.5 %gather_fusion = f32[8192]{0:T(1024)S(1)} fusion(f32[1056]{0:T(1024)S(1)} %reshape.96, s32[8192]{0:T(1024)S(1)} %broadcast_clamp_fusion), kind=kCustom, calls=%fused_computation | custom fusion | bytes 98304 | tf_op jit(solution)/shard_map/jit(_take)/gather | solution.py:128
  198.0 4.1 %collective-permute-start.14 = (f32[53,8,2]{2,1,0:T(8,128)S(1)}, f32[53,8,2]{2,1,0:T(8,128)S(1)}, u32[]{:S(2)}, u32[]{:S(2)}) collective-permute-start(f32[53,8,2]{2,1,0:T(8,128)S(1)} %get-tuple-element.6), channel_id=1, source_target_pairs={{0,1},{1,2},{2,3},{4,5},{5,6},{6,7},{8,9},{9,10},{10,11},{12,13},{... | collective-permute-start | bytes 10184 | tf_op jit(solution)/shard_map/ppermute | solution.py:29
  202.1 1.3 collective-permute-start.15
  203.5 1.4 collective-permute-done.14
  204.9 4.4 %collective-permute-done.15 = f32[53,8,2]{2,1,0:T(8,128)S(1)} collective-permute-done((f32[53,8,2]{2,1,0:T(8,128)S(1)}, f32[53,8,2]{2,1,0:T(8,128)S(1)}, u32[]{:S(2)}, u32[]{:S(2)}) %collective-permute-start.15) | collective-permute-done | bytes 3424 | tf_op jit(solution)/shard_map/ppermute | solution.py:31
  210.2 27.8 %gather_fusion.1 = f32[8192,53]{1,0:T(8,128)} fusion(f32[53,1056]{0,1:T(8,128)S(1)} %copy.18, s32[8192]{0:T(1024)S(1)} %broadcast_clamp_fusion), kind=kCustom, calls=%fused_computation.1 | custom fusion | bytes 3506176 | tf_op jit(solution)/shard_map/jit(_take)/gather | solution.py:127
  238.0 3.9 %copy.19 = f32[8192,53]{0,1:T(8,128)} copy(f32[8192,53]{1,0:T(8,128)} %gather_fusion.1) | data formatting | bytes 3473408 | tf_op jit(solution)/shard_map/jit(_take)/gather | solution.py:127
  241.9 1.8 fusion.16
  243.7 2.0 fusion.14
  245.7 2.0 fusion.9
  247.8 2.0 fusion.4
  249.8 2.0 fusion.13
  251.9 2.0 fusion.8
  253.9 3.3 %fusion.3 = f32[53,8192]{1,0:T(8,128)} fusion(f32[53,8192]{1,0:T(8,128)S(1)} %fusion.8, f32[8192,53]{0,1:T(8,128)S(1)} %fusion.4, f32[53]{0:T(128)S(1)} %compare_convert_fusion, pred[8192]{0:T(1024)(128)(4,1)S(1)} %get-tuple-element.12, f32[3,53,53]{2,1,0:T(8,128)S(1)} %copy-done.4), kind=kOutput, calls=%fused_computation.8 | convolution fusion | flops 277872640 | bytes 5444096 | tf_op jit(solution)/shard_map/dot_general | solution.py:52
  (58 shorter events, 6.1 us)
Async XLA Ops:
  58.6 70.5 %collective-permute-start.8 = (f32[1,2,132]{2,1,0:T(2,128)S(1)}, f32[1,2,132]{2,1,0:T(2,128)S(1)}, u32[]{:S(2)}, u32[]{:S(2)}) collective-permute-start(f32[1,2,132]{2,1,0:T(2,128)S(1)} %get-tuple-element.15), channel_id=1, source_target_pairs={{4,0},{8,4},{12,8},{16,12},{20,16},{24,20},{28,24},{5,1},{9,5},{13... | collective-permute-start | bytes 3176 | tf_op jit(solution)/shard_map/ppermute | solution.py:18
  60.5 69.9 %collective-permute-start.9 = (f32[1,2,132]{2,1,0:T(2,128)S(1)}, f32[1,2,132]{2,1,0:T(2,128)S(1)}, u32[]{:S(2)}, u32[]{:S(2)}) collective-permute-start(f32[1,2,132]{2,1,0:T(2,128)S(1)} %get-tuple-element.16), channel_id=1, source_target_pairs={{0,4},{4,8},{8,12},{12,16},{16,20},{20,24},{24,28},{1,5},{5,9},{9,... | collective-permute-start | bytes 3176 | tf_op jit(solution)/shard_map/ppermute | solution.py:18
  69.4 47.0 %copy-start.6 = (f32[4,128]{1,0:T(4,128)S(1)}, f32[4,128]{1,0:T(4,128)}, u32[]{:S(2)}) copy-start(f32[4,128]{1,0:T(4,128)} %param.13) | copy-start | bytes 6148
  69.4 52.7 %copy-start.5 = (s32[8192]{0:T(1024)S(1)}, s32[8192]{0:T(1024)}, u32[]{:S(2)}) copy-start(s32[8192]{0:T(1024)} %param.11) | copy-start | bytes 98308
  69.4 75.1 %copy-start.2 = (f32[53,4,128]{2,1,0:T(4,128)S(1)}, f32[53,4,128]{2,1,0:T(4,128)}, u32[]{:S(2)}) copy-start(f32[53,4,128]{2,1,0:T(4,128)} %param.12) | copy-start | bytes 325636
  114.5 17.3 %collective-permute-start.4 = (f32[53,2,132]{2,1,0:T(2,128)S(1)}, f32[53,2,132]{2,1,0:T(2,128)S(1)}, u32[]{:S(2)}, u32[]{:S(2)}) collective-permute-start(f32[53,2,132]{2,1,0:T(2,128)S(1)} %get-tuple-element.4), channel_id=1, source_target_pairs={{4,0},{8,4},{12,8},{16,12},{20,16},{24,20},{28,24},{5,1},{9,5},{13... | collective-permute-start | bytes 167912 | tf_op jit(solution)/shard_map/ppermute | solution.py:18
  116.5 5.7 %collective-permute-start = (f32[1,2,128]{2,1,0:T(2,128)S(1)}, f32[1,2,128]{2,1,0:T(2,128)S(1)}, u32[]{:S(2)}, u32[]{:S(2)}) collective-permute-start(f32[1,2,128]{2,1,0:T(2,128)S(1)} %get-tuple-element.21), channel_id=1, source_target_pairs={{0,4},{4,8},{8,12},{12,16},{16,20},{20,24},{24,28},{1,5},{5,9},{9,... | collective-permute-start | bytes 3080 | tf_op jit(solution)/shard_map/ppermute | solution.py:29
  120.1 5.7 %collective-permute-start.1 = (f32[1,2,128]{2,1,0:T(2,128)S(1)}, f32[1,2,128]{2,1,0:T(2,128)S(1)}, u32[]{:S(2)}, u32[]{:S(2)}) collective-permute-start(f32[1,2,128]{2,1,0:T(2,128)S(1)} %get-tuple-element.22), channel_id=1, source_target_pairs={{4,0},{8,4},{12,8},{16,12},{20,16},{24,20},{28,24},{5,1},{9,5},{13... | collective-permute-start | bytes 3080 | tf_op jit(solution)/shard_map/ppermute | solution.py:31
  122.2 14.3 %collective-permute-start.5 = (f32[53,2,132]{2,1,0:T(2,128)S(1)}, f32[53,2,132]{2,1,0:T(2,128)S(1)}, u32[]{:S(2)}, u32[]{:S(2)}) collective-permute-start(f32[53,2,132]{2,1,0:T(2,128)S(1)} %get-tuple-element.5), channel_id=1, source_target_pairs={{0,4},{4,8},{8,12},{12,16},{16,20},{20,24},{24,28},{1,5},{5,9},{9,... | collective-permute-start | bytes 167912 | tf_op jit(solution)/shard_map/ppermute | solution.py:18
  125.9 26.1 %collective-permute-start.2 = (f32[1,8,2]{2,1,0:T(8,128)S(1)}, f32[1,8,2]{2,1,0:T(8,128)S(1)}, u32[]{:S(2)}, u32[]{:S(2)}) collective-permute-start(f32[1,8,2]{2,1,0:T(8,128)S(1)} %get-tuple-element.17), channel_id=1, source_target_pairs={{0,1},{1,2},{2,3},{4,5},{5,6},{6,7},{8,9},{9,10},{10,11},{12,13},{... | collective-permute-start | bytes 200 | tf_op jit(solution)/shard_map/ppermute | solution.py:29
  129.1 22.9 %collective-permute-start.3 = (f32[1,8,2]{2,1,0:T(8,128)S(1)}, f32[1,8,2]{2,1,0:T(8,128)S(1)}, u32[]{:S(2)}, u32[]{:S(2)}) collective-permute-start(f32[1,8,2]{2,1,0:T(8,128)S(1)} %get-tuple-element.18), channel_id=1, source_target_pairs={{1,0},{2,1},{3,2},{5,4},{6,5},{7,6},{9,8},{10,9},{11,10},{13,12},{... | collective-permute-start | bytes 200 | tf_op jit(solution)/shard_map/ppermute | solution.py:31
  130.5 7.5 %collective-permute-start.10 = (f32[1,4,2]{2,1,0:T(4,128)S(1)}, f32[1,4,2]{2,1,0:T(4,128)S(1)}, u32[]{:S(2)}, u32[]{:S(2)}) collective-permute-start(f32[1,4,2]{2,1,0:T(4,128)S(1)} %get-tuple-element.19), channel_id=1, source_target_pairs={{1,0},{2,1},{3,2},{5,4},{6,5},{7,6},{9,8},{10,9},{11,10},{13,12},{... | collective-permute-start | bytes 104 | tf_op jit(solution)/shard_map/ppermute | solution.py:18
  131.8 10.2 %collective-permute-start.11 = (f32[1,4,2]{2,1,0:T(4,128)S(1)}, f32[1,4,2]{2,1,0:T(4,128)S(1)}, u32[]{:S(2)}, u32[]{:S(2)}) collective-permute-start(f32[1,4,2]{2,1,0:T(4,128)S(1)} %get-tuple-element.20), channel_id=1, source_target_pairs={{0,1},{1,2},{2,3},{4,5},{5,6},{6,7},{8,9},{9,10},{10,11},{12,13},{... | collective-permute-start | bytes 104 | tf_op jit(solution)/shard_map/ppermute | solution.py:18
  136.7 6.9 %collective-permute-start.6 = (f32[53,4,2]{2,1,0:T(4,128)S(1)}, f32[53,4,2]{2,1,0:T(4,128)S(1)}, u32[]{:S(2)}, u32[]{:S(2)}) collective-permute-start(f32[53,4,2]{2,1,0:T(4,128)S(1)} %get-tuple-element.8), channel_id=1, source_target_pairs={{1,0},{2,1},{3,2},{5,4},{6,5},{7,6},{9,8},{10,9},{11,10},{13,12},{... | collective-permute-start | bytes 5096 | tf_op jit(solution)/shard_map/ppermute | solution.py:18
  138.1 6.5 %collective-permute-start.7 = (f32[53,4,2]{2,1,0:T(4,128)S(1)}, f32[53,4,2]{2,1,0:T(4,128)S(1)}, u32[]{:S(2)}, u32[]{:S(2)}) collective-permute-start(f32[53,4,2]{2,1,0:T(4,128)S(1)} %get-tuple-element.9), channel_id=1, source_target_pairs={{0,1},{1,2},{2,3},{4,5},{5,6},{6,7},{8,9},{9,10},{10,11},{12,13},{... | collective-permute-start | bytes 5096 | tf_op jit(solution)/shard_map/ppermute | solution.py:18
  144.7 64.6 %copy-start.1 = (f32[53,4,128]{2,1,0:T(4,128)}, f32[53,4,128]{2,1,0:T(4,128)S(1)}, u32[]{:S(2)}) copy-start(f32[53,4,128]{2,1,0:T(4,128)S(1)} %fusion.28) | copy-start | bytes 325636
  144.8 53.0 %collective-permute-start.12 = (f32[53,2,128]{2,1,0:T(2,128)S(1)}, f32[53,2,128]{2,1,0:T(2,128)S(1)}, u32[]{:S(2)}, u32[]{:S(2)}) collective-permute-start(f32[53,2,128]{2,1,0:T(2,128)S(1)} %get-tuple-element.10), channel_id=1, source_target_pairs={{0,4},{4,8},{8,12},{12,16},{16,20},{20,24},{24,28},{1,5},{5,9},{9,... | collective-permute-start | bytes 162824 | tf_op jit(solution)/shard_map/ppermute | solution.py:29
  150.1 47.7 %collective-permute-start.13 = (f32[53,2,128]{2,1,0:T(2,128)S(1)}, f32[53,2,128]{2,1,0:T(2,128)S(1)}, u32[]{:S(2)}, u32[]{:S(2)}) collective-permute-start(f32[53,2,128]{2,1,0:T(2,128)S(1)} %get-tuple-element.11), channel_id=1, source_target_pairs={{4,0},{8,4},{12,8},{16,12},{20,16},{24,20},{28,24},{5,1},{9,5},{13... | collective-permute-start | bytes 162824 | tf_op jit(solution)/shard_map/ppermute | solution.py:31
  198.0 6.9 %collective-permute-start.14 = (f32[53,8,2]{2,1,0:T(8,128)S(1)}, f32[53,8,2]{2,1,0:T(8,128)S(1)}, u32[]{:S(2)}, u32[]{:S(2)}) collective-permute-start(f32[53,8,2]{2,1,0:T(8,128)S(1)} %get-tuple-element.6), channel_id=1, source_target_pairs={{0,1},{1,2},{2,3},{4,5},{5,6},{6,7},{8,9},{9,10},{10,11},{12,13},{... | collective-permute-start | bytes 10184 | tf_op jit(solution)/shard_map/ppermute | solution.py:29
  202.1 7.2 %collective-permute-start.15 = (f32[53,8,2]{2,1,0:T(8,128)S(1)}, f32[53,8,2]{2,1,0:T(8,128)S(1)}, u32[]{:S(2)}, u32[]{:S(2)}) collective-permute-start(f32[53,8,2]{2,1,0:T(8,128)S(1)} %get-tuple-element.7), channel_id=1, source_target_pairs={{1,0},{2,1},{3,2},{5,4},{6,5},{7,6},{9,8},{10,9},{11,10},{13,12},{... | collective-permute-start | bytes 10184 | tf_op jit(solution)/shard_map/ppermute | solution.py:31
  238.0 3.9 %copy-start = (f32[53,8192]{1,0:T(8,128)S(1)}, f32[53,8192]{1,0:T(8,128)}, u32[]{:S(2)}) copy-start(f32[53,8192]{1,0:T(8,128)} %param.8) | copy-start | bytes 5210116
  241.9 1.8 copy-start.3
  247.8 2.0 copy-start.4
where the time goes:
time: 260 us; the launch traced here: 257 us
  other arithmetic  107 us (41%)
  local copies, waits for them, and re-layouts  81.6 us (31%)
  starting transfers between devices  45.8 us (18%)
  matrix products  13.4 us (5%)
  waiting for transfers between devices  8.17 us (3%)
    scatter-add x1, other arithmetic, per_device(): jnp.zeros((1, span_x * span_y), jnp.float32).at[:, ext_index]  56.9 us
    gather x1, local copies, waits for them, and re-layouts, per_device(): jnp.take(ext_rate.reshape(span_x * span_y), ext_index, axis=0)  45.5 us
    scatter-add x1, other arithmetic, per_device(): jnp.zeros((species_count, span_x * span_y), jnp.float32).at[:, ext_index]  44.5 us
    gather x2, local copies, waits for them, and re-layouts, per_device(): jnp.take(ext_means.reshape(species_count, span_x * span_y), ext_index, ax...  31.7 us
    ppermute x8, starting transfers between devices, from_behind(): lax.ppermute(value, axis, [(source, source + steps) for source in range(l...  23.2 us
    ppermute x4, starting transfers between devices, padded(): lax.ppermute(tail, axis, [(i, (i + 1) % count) for i in range(ends)])  16.3 us
    dot_general x3, matrix products, react_padded(): jnp.dot(implicit_map[tier_index], source, precision=lax.Precision.HIGHEST...  7.35 us
    ppermute x4, starting transfers between devices, padded(): lax.ppermute(head, axis, [((i + 1) % count, i) for i in range(ends)])  6.43 us
  transfers between devices with their start and end apart: 16, of which 4 were waited for; matrix products, arithmetic and copies ran while one was open for 37% of the time, Pallas kernels for 0%

commit v1 on v0

v1 whole, which is shorter than its diff:
```python
import functools

import jax
import jax.numpy as jnp
from jax import lax
from jax.experimental import pallas as pl
from jax.experimental.pallas import tpu as pltpu
from jax.sharding import PartitionSpec as P

NS_LOW = 21
NS_MID = 24
R = 2
W = 2 * R
HALF = 64
ROWS = 56
LANES = 128

prior_weight = 16.0
chem_step = 0.5
BF = jnp.bfloat16
F32 = jnp.float32
MESH = pl.DeviceIdType.MESH


def halves(value):
    high = value.astype(BF)
    return high, (value - high.astype(F32)).astype(BF)


def roll(value, shift):
    return pltpu.roll(value, shift % value.shape[1], 1)


def fill_one_hot(one_hot, cell, block_x, block_y):
    span_x = block_x + 2 * R
    count = cell.shape[1]
    local_x = cell[0:1] - (lax.axis_index("gx") * block_x - R)
    local_y = cell[1:2] - (lax.axis_index("gy") * block_y - R)
    low_rim = local_y < W
    high_rim = local_y >= block_y
    rim = jnp.where(low_rim, local_y, local_y - block_y + span_x * W) + local_x * W
    inner = jnp.where(low_rim | high_rim, -1, local_y - R)
    rim = jnp.where(low_rim | high_rim, rim, -1)
    sub = lax.broadcasted_iota(jnp.int32, (block_y, count), 0)
    hot_y = jnp.where(sub == inner, 1.0, 0.0).astype(BF)
    for x in range(span_x):
        hot_x = jnp.broadcast_to(jnp.where(local_x == x, 1.0, 0.0), (block_y, count))
        one_hot[x * block_y : (x + 1) * block_y, :] = hot_y * hot_x.astype(BF)
    sub = lax.broadcasted_iota(jnp.int32, (LANES, count), 0)
    one_hot[span_x * block_y : span_x * block_y + LANES, :] = jnp.where(
        sub == rim, 1.0, 0.0
    ).astype(BF)


def scatter_kernel(block_x, block_y, comp, mass, cell, sums, one_hot, weighted):
    species = comp.shape[0]

    @pl.when(pl.program_id(0) == 0)
    def _():
        sums[...] = jnp.zeros_like(sums)
        weighted[...] = jnp.zeros_like(weighted)

    weighted[0:species, :] = comp[...] * mass[...]
    weighted[species : species + 1, :] = mass[...]
    high, low = halves(weighted[...])
    fill_one_hot(one_hot, cell[...], block_x, block_y)
    sums[...] += lax.dot_general(
        jnp.concatenate([high, low], 0),
        one_hot[...],
        (((1,), (1,)), ((), ())),
        preferred_element_type=F32,
    )


def exchange_kernel(
    counts, species, block_x, block_y, sums, les, rate, table, means,
    send, own, from_x, from_y, from_xy, wide, send_main, recv_main, send_rim, recv_rim,
):
    span_x = block_x + 2 * R
    gx, gy = lax.axis_index("gx"), lax.axis_index("gy")
    has = {
        -1: (gx > 0, gy > 0),
        1: (gx < counts[0] - 1, gy < counts[1] - 1),
        0: (True, True),
    }
    others = [(dx, dy) for dx in (-1, 0, 1) for dy in (-1, 0, 1) if (dx, dy) != (0, 0)]

    def present(dx, dy):
        return jnp.logical_and(has[dx][0], has[dy][1])

    barrier = pltpu.get_barrier_semaphore()
    for dx, dy in others:
        @pl.when(present(dx, dy))
        def _():
            pl.semaphore_signal(
                barrier, inc=1, device_id=(gx + dx, gy + dy), device_id_type=MESH
            )

    lane = lax.broadcasted_iota(jnp.int32, (ROWS, LANES), 1)
    lane_y = lax.broadcasted_iota(jnp.int32, (ROWS, block_y), 1)
    inside = (lane_y >= R) & (lane_y < block_y - R)
    for x in range(span_x + 1):
        at = x * block_y
        width = block_y if x < span_x else LANES
        send[x] = sums[0:ROWS, at : at + width] + sums[HALF : HALF + ROWS, at : at + width]
    own[...] = jnp.zeros_like(own)
    rim_prior = jnp.zeros((ROWS, LANES), F32)
    for x in range(block_x):
        t = x + R
        own[0:species, :] = prior_weight * les[:, x, :]
        own[species : species + 1, :] = jnp.full((1, block_y), prior_weight, F32)
        own[species + 1 : species + 2, :] = 1.0 - jnp.exp(-rate[x : x + 1, :])
        prior = own[...]
        send[t] += jnp.where(inside, prior, 0.0)
        low_at, high_at = t * W + R, (span_x + t) * W
        low = roll(prior, low_at)
        high = roll(prior, high_at + R)
        rim_prior += jnp.where((lane >= low_at) & (lane < low_at + R), low, 0.0)
        rim_prior += jnp.where((lane >= high_at) & (lane < high_at + R), high, 0.0)
    send[span_x] += rim_prior

    number = (1 + (gx > 0).astype(jnp.int32) + (gx < counts[0] - 1).astype(jnp.int32)) * (
        1 + (gy > 0).astype(jnp.int32) + (gy < counts[1] - 1).astype(jnp.int32)
    ) - 1
    pl.semaphore_wait(barrier, number)

    def landing(dx, dy):
        if dy == 0:
            return from_x.at[(dx + 1) // 2, W]
        if dx == 0:
            return from_y.at[(dy + 1) // 2]
        return from_xy.at[(dx + 1) // 2, (dy + 1) // 2]

    def main_copy(dx):
        first = 0 if dx < 0 else block_x
        return pltpu.make_async_remote_copy(
            src_ref=send.at[pl.ds(first, W)],
            dst_ref=from_x.at[(1 - dx) // 2, pl.ds(0, W)],
            send_sem=send_main.at[(dx + 1) // 2],
            recv_sem=recv_main.at[(1 - dx) // 2],
            device_id=(gx + dx, gy),
            device_id_type=MESH,
        )

    def rim_copy(k, dx, dy):
        return pltpu.make_async_remote_copy(
            src_ref=send.at[span_x],
            dst_ref=landing(-dx, -dy),
            send_sem=send_rim.at[k],
            recv_sem=recv_rim.at[len(others) - 1 - k],
            device_id=(gx + dx, gy + dy),
            device_id_type=MESH,
        )

    for k, (dx, dy) in enumerate(others):
        @pl.when(present(dx, dy))
        def _():
            rim_copy(k, dx, dy).start()
    for dx in (-1, 1):
        @pl.when(has[dx][0])
        def _():
            main_copy(dx).start()

        @pl.when(jnp.logical_not(has[dx][0]))
        def _():
            from_x[(dx + 1) // 2] = jnp.zeros((W + 1, ROWS, LANES), F32)
    for dx, dy in others:
        if dy != 0:
            @pl.when(jnp.logical_not(present(dx, dy)))
            def _():
                landing(dx, dy)[...] = jnp.zeros((ROWS, LANES), F32)

    for k, (dx, dy) in enumerate(others):
        @pl.when(present(dx, dy))
        def _():
            pltpu.make_async_remote_copy(
                src_ref=send.at[span_x],
                dst_ref=landing(dx, dy),
                send_sem=send_rim.at[k],
                recv_sem=recv_rim.at[k],
                device_id=(gx + dx, gy + dy),
                device_id_type=MESH,
            ).wait_recv()
    for dx in (-1, 1):
        @pl.when(has[dx][0])
        def _():
            pltpu.make_async_remote_copy(
                src_ref=send.at[pl.ds(0, W)],
                dst_ref=from_x.at[(dx + 1) // 2, pl.ds(0, W)],
                send_sem=send_main.at[(dx + 1) // 2],
                recv_sem=recv_main.at[(dx + 1) // 2],
                device_id=(gx + dx, gy),
                device_id_type=MESH,
            ).wait_recv()

    row = lax.broadcasted_iota(jnp.int32, (ROWS, LANES), 0)
    wide[...] = jnp.zeros_like(wide)

    def finish(total, x):
        mass = total[species : species + 1, :]
        weight = jnp.broadcast_to(jnp.where(mass > 0.0, mass, 1.0), total.shape)
        value = total / jnp.where(row < species, weight, 1.0)
        wide[0:ROWS, :] = value
        high, low = halves(wide[...])
        table[0:HALF, x * block_y : x * block_y + LANES] = high
        table[HALF:, x * block_y : x * block_y + LANES] = low
        return value

    side_size = span_x * W
    low_side = lane < side_size
    place_x = jnp.where(low_side, lane, lane - side_size)
    used = lane < 2 * side_size
    behind = used & (place_x < 2 * R * W)
    ahead = used & (place_x >= block_x * W)
    step = block_x * W
    total = send[span_x]
    for dx in (-1, 0, 1):
        for dy in (-1, 0, 1):
            if (dx, dy) == (0, 0):
                continue
            mask = used if dx == 0 else behind if dx < 0 else ahead
            if dy != 0:
                mask = mask & (low_side if dy < 0 else jnp.logical_not(low_side))
            shift = dx * step + dy * side_size
            total = total + jnp.where(mask, roll(landing(dx, dy)[...], shift), 0.0)
    rim_value = finish(total, span_x)
    for t in range(span_x):
        total = send[t]
        if t < W:
            total = total + from_x[0, t]
        if t >= block_x:
            total = total + from_x[1, t - block_x]
        value = finish(total, t)
        if R <= t < R + block_x:
            low_at, high_at = t * W + R, (span_x + t) * W
            value = jnp.where(lane_y < R, roll(rim_value, -low_at), value)
            value = jnp.where(
                lane_y >= block_y - R, roll(rim_value, block_y - R - high_at), value
            )
            means[:, t - R, :] = value[0:species]

    for k, (dx, dy) in enumerate(others):
        @pl.when(present(dx, dy))
        def _():
            rim_copy(k, dx, dy).wait_send()
    for dx in (-1, 1):
        @pl.when(has[dx][0])
        def _():
            main_copy(dx).wait_send()


def stack_levels(target, plain, matrices):
    species = matrices.shape[1]
    plain[...] = jnp.zeros_like(plain)
    plain[0:species, 0:species] = matrices[2]
    plain[HALF : HALF + NS_MID, 0:NS_MID] = matrices[1, 0:NS_MID, 0:NS_MID]
    base = HALF + NS_MID
    plain[base : base + NS_LOW, 0:NS_LOW] = matrices[0, 0:NS_LOW, 0:NS_LOW]
    high, low = halves(plain[...])
    target[:, 0:HALF] = high
    target[:, HALF : 2 * HALF] = high
    target[:, 2 * HALF :] = low


def react_kernel(
    block_x, block_y, comp, cell, level, table, rate, implicit, out,
    one_hot, mixed, plain, left_rate, left_implicit,
):
    species = comp.shape[0]

    @pl.when(pl.program_id(0) == 0)
    def _():
        mixed[...] = jnp.zeros_like(mixed)
        stack_levels(left_rate, plain, rate)
        stack_levels(left_implicit, plain, implicit)

    fill_one_hot(one_hot, cell[...], block_x, block_y)
    both = jnp.dot(table[...], one_hot[...], preferred_element_type=F32)
    taken = both[0:HALF] + both[HALF:]
    factor = taken[species + 1 : species + 2]
    comp_value = comp[...]
    mixed[0:species, :] = comp_value - factor * (comp_value - taken[0:species])
    levels = level[...]
    full, middle = levels == 2, levels == 1
    high, low = halves(mixed[...])
    right = jnp.concatenate([high, low, high], 0)
    drive = jnp.dot(left_rate[...], right, preferred_element_type=F32)
    base = HALF + NS_MID
    top = jnp.where(
        full, drive[0:NS_MID],
        jnp.where(middle, drive[HALF:base], drive[base : base + NS_MID]),
    )
    source = jnp.tanh(jnp.concatenate([top, drive[NS_MID:HALF]], 0))
    high, low = halves(source)
    right = jnp.concatenate([high, low, high], 0)
    change = jnp.dot(left_implicit[...], right, preferred_element_type=F32)
    top = jnp.where(
        full, change[0:NS_MID],
        jnp.where(middle, change[HALF:base], change[base : base + NS_MID]),
    )
    rest = jnp.where(full, change[NS_MID:species], 0.0)
    out[0:NS_MID, :] = mixed[0:NS_MID, :] + chem_step * top
    out[NS_MID:, :] = mixed[NS_MID:species, :] + chem_step * rest


def per_device(
    counts, composition, particle_mass, particle_cell, particle_level,
    les_mean, mix_rate, rate_matrix, implicit_map,
):
    species, particles = composition.shape
    block_x, block_y = les_mean.shape[1], les_mean.shape[2]
    span_x = block_x + 2 * R
    columns = span_x * block_y + LANES
    chunk = 1024
    steps = particles // chunk
    whole = pl.BlockSpec(memory_space=pltpu.VMEM)

    def by_chunk(rows):
        return pl.BlockSpec((rows, chunk), lambda i: (0, i))

    params = pltpu.CompilerParams(vmem_limit_bytes=48 << 20)
    sums = pl.pallas_call(
        functools.partial(scatter_kernel, block_x, block_y),
        grid=(steps,),
        out_shape=jax.ShapeDtypeStruct((2 * HALF, columns), F32),
        in_specs=[by_chunk(species), by_chunk(1), by_chunk(2)],
        out_specs=pl.BlockSpec((2 * HALF, columns), lambda i: (0, 0)),
        scratch_shapes=[pltpu.VMEM((columns, chunk), BF), pltpu.VMEM((HALF, chunk), F32)],
        compiler_params=params,
    )(composition, particle_mass[None], particle_cell)
    dma = pltpu.SemaphoreType.DMA
    table, means = pl.pallas_call(
        functools.partial(exchange_kernel, counts, species, block_x, block_y),
        out_shape=(
            jax.ShapeDtypeStruct((2 * HALF, columns), BF),
            jax.ShapeDtypeStruct(les_mean.shape, F32),
        ),
        in_specs=[whole] * 3,
        out_specs=(whole, whole),
        scratch_shapes=[
            pltpu.VMEM((span_x + 1, ROWS, LANES), F32),
            pltpu.VMEM((ROWS, block_y), F32),
            pltpu.VMEM((2, W + 1, ROWS, LANES), F32),
            pltpu.VMEM((2, ROWS, LANES), F32),
            pltpu.VMEM((2, 2, ROWS, LANES), F32),
            pltpu.VMEM((HALF, LANES), F32),
            dma((2,)), dma((2,)), dma((8,)), dma((8,)),
        ],
        compiler_params=pltpu.CompilerParams(collective_id=0, has_side_effects=True),
    )(sums, les_mean, mix_rate)
    stacked = HALF + 2 * NS_MID
    updated = pl.pallas_call(
        functools.partial(react_kernel, block_x, block_y),
        grid=(steps,),
        out_shape=jax.ShapeDtypeStruct(composition.shape, F32),
        in_specs=[by_chunk(species), by_chunk(2), by_chunk(1), whole, whole, whole],
        out_specs=by_chunk(species),
        scratch_shapes=[
            pltpu.VMEM((columns, chunk), BF),
            pltpu.VMEM((HALF, chunk), F32),
            pltpu.VMEM((stacked, HALF), F32),
            pltpu.VMEM((stacked, 3 * HALF), BF),
            pltpu.VMEM((stacked, 3 * HALF), BF),
        ],
        compiler_params=params,
    )(composition, particle_cell, particle_level[None], table, rate_matrix, implicit_map)
    return updated, means


def solution(mesh):
    placed = (
        P(None, ("gx", "gy")),
        P(("gx", "gy")),
        P(None, ("gx", "gy")),
        P(("gx", "gy")),
        P(None, "gx", "gy"),
        P("gx", "gy"),
        P(),
        P(),
    )
    return jax.shard_map(
        functools.partial(per_device, (mesh.shape["gx"], mesh.shape["gy"])),
        mesh=mesh,
        in_specs=placed,
        out_specs=(P(None, ("gx", "gy")), P(None, "gx", "gy")),
        check_vma=False,
    )
```

time: 260 us -> 34.6 us (0.13)
  the two profiles are of different devices: /device:TPU:1 before, /device:TPU:19 now
where the time goes in v1:
time: 34.6 us; the launch traced here: 34.3 us
  Pallas kernels  28 us (81%)
  local copies, waits for them, and re-layouts  5.52 us (16%)
  between operations  0.73 us (2%)
    pallas_call x1, Pallas kernels, per_device(): pl.pallas_call(functools.partial(exchange_kernel, counts, species, block_...  11.5 us
    pallas_call x1, Pallas kernels, per_device(): pl.pallas_call(functools.partial(react_kernel, block_x, block_y), grid=(s...  8.86 us
    pallas_call x1, Pallas kernels, per_device(): pl.pallas_call(functools.partial(scatter_kernel, block_x, block_y), grid=...  7.69 us
    unnamed x23, local copies, waits for them, and re-layouts  5.52 us

profile of v1, /device:TPU:19, one launch (start us, length us, event | category | flops | bytes accessed | tf_op | source)
XLA Modules:
  0.0 34.3 jit_solution(8902186210643170180)
XLA Ops:
  0.6 0.0 copy-start
  0.6 1.5 %copy-done = f32[53,8192]{1,0:T(8,128)S(1)} copy-done((f32[53,8192]{1,0:T(8,128)S(1)}, f32[53,8192]{1,0:T(8,128)}, u32[]{:S(2)}) %copy-start) | copy-done | bytes 1736728
  2.1 0.0 copy-start.4
  2.1 0.8 %copy-done.4 = s32[2,8192]{1,0:T(2,128)S(1)} copy-done((s32[2,8192]{1,0:T(2,128)S(1)}, s32[2,8192]{1,0:T(2,128)}, u32[]{:S(2)}) %copy-start.4) | copy-done | bytes 65560
  3.0 0.0 copy-start.8
  3.0 0.8 %copy-done.8 = f32[8192]{0:T(1024)S(1)} copy-done((f32[8192]{0:T(1024)S(1)}, f32[8192]{0:T(1024)}, u32[]{:S(2)}) %copy-start.8) | copy-done | bytes 32792
  3.7 0.0 copy-start.1
  3.7 0.0 copy-start.5
  3.7 0.0 copy-start.6
  3.7 0.0 copy-start.7
  3.7 0.0 copy-start.9
  3.8 7.7 %shard_map.95.sums = f32[128,1152]{1,0:T(8,128)S(1)} custom-call(f32[53,8192]{1,0:T(8,128)S(1)} %copy-done, f32[1,8192]{1,0:T(1,128)S(1)} %bitcast.2, s32[2,8192]{1,0:T(2,128)S(1)} %copy-done.4), custom_call_target="tpu_custom_call" | custom-call | tf_op jit(solution)/shard_map/pallas_call | solution.py:322
  11.4 0.0 copy-start.2
  11.5 0.8 %copy-done.2 = f32[128,1152]{1,0:T(8,128)} copy-done((f32[128,1152]{1,0:T(8,128)}, f32[128,1152]{1,0:T(8,128)S(1)}, u32[]{:S(2)}) %copy-start.2) | copy-done | bytes 589848
  12.3 11.5 %shard_map.96 = (bf16[128,1152]{1,0:T(8,128)(2,1)}, f32[53,4,128]{2,1,0:T(4,128)}) custom-call(f32[128,1152]{1,0:T(8,128)} %copy-done.2, f32[53,4,128]{2,1,0:T(4,128)} %les.1, f32[4,128]{1,0:T(4,128)} %rate.2), custom_call_target="tpu_custom_call" | custom-call | tf_op jit(solution)/shard_map/pallas_call | solution.py:332
  23.7 0.0 copy-done.1
  23.7 0.0 copy-done.5
  23.8 0.0 copy-done.6
  23.8 0.0 copy-done.7
  23.8 0.0 copy-done.9
  23.8 0.0 copy-start.3
  23.8 1.0 %copy-done.3 = bf16[128,1152]{1,0:T(8,128)(2,1)S(1)} copy-done((bf16[128,1152]{1,0:T(8,128)(2,1)S(1)}, bf16[128,1152]{1,0:T(8,128)(2,1)}, u32[]{:S(2)}) %copy-start.3) | copy-done | bytes 294936
  24.7 0.0 copy-start.10
  24.8 8.9 %shard_map.97 = f32[53,8192]{1,0:T(8,128)} custom-call(f32[53,8192]{1,0:T(8,128)S(1)} %copy-done.1, s32[2,8192]{1,0:T(2,128)S(1)} %copy-done.5, s32[1,8192]{1,0:T(1,128)S(1)} %bitcast.3, bf16[128,1152]{1,0:T(8,128)(2,1)S(1)} %copy-done.3, f32[3,53,53]{2,1,0:T(8,128)S(1)} %copy-done.6, f32[3,53,53]{2,1,0:T(8,128)S(1)} %copy-done.7), custom_call_target="tpu_custom_call" | custom-call | tf_op jit(solution)/shard_map/pallas_call | solution.py:352
  33.6 0.0 copy-done.10
  33.6 0.6 %copy.11 = f32[53,4,128]{2,1,0:T(4,128)} copy(f32[53,4,128]{2,1,0:T(4,128)S(1)} %copy-done.10) | data formatting | bytes 217088
Async XLA Ops:
  0.6 1.5 %copy-start = (f32[53,8192]{1,0:T(8,128)S(1)}, f32[53,8192]{1,0:T(8,128)}, u32[]{:S(2)}) copy-start(f32[53,8192]{1,0:T(8,128)} %comp.3) | copy-start | bytes 5210116
  2.1 0.8 %copy-start.4 = (s32[2,8192]{1,0:T(2,128)S(1)}, s32[2,8192]{1,0:T(2,128)}, u32[]{:S(2)}) copy-start(s32[2,8192]{1,0:T(2,128)} %cell.3) | copy-start | bytes 196612
  3.0 0.8 %copy-start.8 = (f32[8192]{0:T(1024)S(1)}, f32[8192]{0:T(1024)}, u32[]{:S(2)}) copy-start(f32[8192]{0:T(1024)} %param.9) | copy-start | bytes 98308
  3.7 20.0 %copy-start.1 = (f32[53,8192]{1,0:T(8,128)S(1)}, f32[53,8192]{1,0:T(8,128)}, u32[]{:S(2)}) copy-start(f32[53,8192]{1,0:T(8,128)} %comp.3) | copy-start | bytes 5210116
  3.7 20.0 %copy-start.5 = (s32[2,8192]{1,0:T(2,128)S(1)}, s32[2,8192]{1,0:T(2,128)}, u32[]{:S(2)}) copy-start(s32[2,8192]{1,0:T(2,128)} %cell.3) | copy-start | bytes 196612
  3.7 20.0 %copy-start.6 = (f32[3,53,53]{2,1,0:T(8,128)S(1)}, f32[3,53,53]{2,1,0:T(8,128)}, u32[]{:S(2)}) copy-start(f32[3,53,53]{2,1,0:T(8,128)} %rate.3) | copy-start | bytes 101128
  3.7 20.0 %copy-start.7 = (f32[3,53,53]{2,1,0:T(8,128)S(1)}, f32[3,53,53]{2,1,0:T(8,128)}, u32[]{:S(2)}) copy-start(f32[3,53,53]{2,1,0:T(8,128)} %implicit.1) | copy-start | bytes 101128
  3.7 20.0 %copy-start.9 = (s32[8192]{0:T(1024)S(1)}, s32[8192]{0:T(1024)}, u32[]{:S(2)}) copy-start(s32[8192]{0:T(1024)} %param.11) | copy-start | bytes 98308
  11.4 0.8 %copy-start.2 = (f32[128,1152]{1,0:T(8,128)}, f32[128,1152]{1,0:T(8,128)S(1)}, u32[]{:S(2)}) copy-start(f32[128,1152]{1,0:T(8,128)S(1)} %shard_map.95.sums) | copy-start | bytes 1769476
  23.8 1.0 %copy-start.3 = (bf16[128,1152]{1,0:T(8,128)(2,1)S(1)}, bf16[128,1152]{1,0:T(8,128)(2,1)}, u32[]{:S(2)}) copy-start(bf16[128,1152]{1,0:T(8,128)(2,1)} %get-tuple-element.4.table) | copy-start | bytes 884740
  24.7 8.9 %copy-start.10 = (f32[53,4,128]{2,1,0:T(4,128)S(1)}, f32[53,4,128]{2,1,0:T(4,128)}, u32[]{:S(2)}) copy-start(f32[53,4,128]{2,1,0:T(4,128)} %get-tuple-element.9) | copy-start | bytes 325636

commit v2 on v1

v2 whole, which is shorter than its diff:
```python
import functools

import jax
import jax.numpy as jnp
from jax import lax
from jax.experimental import pallas as pl
from jax.experimental.pallas import tpu as pltpu
from jax.sharding import PartitionSpec as P

NS_LOW = 21
NS_MID = 24
R = 2
W = 2 * R
HALF = 64
ROWS = 56
LANES = 128

prior_weight = 16.0
chem_step = 0.5
BF = jnp.bfloat16
F32 = jnp.float32
MESH = pl.DeviceIdType.MESH


def halves(value):
    high = value.astype(BF)
    return high, (value - high.astype(F32)).astype(BF)


def roll(value, shift):
    return pltpu.roll(value, shift % value.shape[1], 1)


def positions(cell, block_x, block_y):
    local_x = cell[0:1] - (lax.axis_index("gx") * block_x - R)
    local_y = cell[1:2] - (lax.axis_index("gy") * block_y - R)
    low_rim = local_y < W
    on_rim = low_rim | (local_y >= block_y)
    rim = jnp.where(low_rim, local_y, local_y - block_y + (block_x + 2 * R) * W) + local_x * W
    return local_x, jnp.where(on_rim, -1, local_y - R), jnp.where(on_rim, rim, -1)


def one_hot(place, rows, period):
    sub = lax.broadcasted_iota(jnp.int32, (rows, place.shape[1]), 0)
    if period < rows:
        sub = sub % period
    return jnp.where(sub == place, 1.0, 0.0).astype(BF)


def sums_kernel(
    counts, steps, chunk, block_x, block_y, comp, mass, cell, les, rate, table, means,
    hot, hot_rim, weighted, split, acc, acc_rim,
    send, prior, from_x, from_y, from_xy, send_main, recv_main, send_rim, recv_rim,
):
    species = comp.shape[0]
    span_x = block_x + 2 * R
    side_size = span_x * W
    gx, gy = lax.axis_index("gx"), lax.axis_index("gy")
    index = pl.program_id(0)
    has = {
        -1: (gx > 0, gy > 0),
        1: (gx < counts[0] - 1, gy < counts[1] - 1),
        0: (True, True),
    }
    others = [(dx, dy) for dx in (-1, 0, 1) for dy in (-1, 0, 1) if (dx, dy) != (0, 0)]
    lane = lax.broadcasted_iota(jnp.int32, (ROWS, LANES), 1)
    row = lax.broadcasted_iota(jnp.int32, (ROWS, LANES), 0)
    inside = (lane >= R) & (lane < block_y - R)

    def present(dx, dy):
        return jnp.logical_and(has[dx][0], has[dy][1])

    def landing(dx, dy):
        if dy == 0:
            return from_x.at[(dx + 1) // 2, W]
        if dx == 0:
            return from_y.at[(dy + 1) // 2]
        return from_xy.at[(dx + 1) // 2, (dy + 1) // 2]

    def main_copy(dx):
        first = 0 if dx < 0 else block_x
        return pltpu.make_async_remote_copy(
            src_ref=send.at[pl.ds(first, W)],
            dst_ref=from_x.at[(1 - dx) // 2, pl.ds(0, W)],
            send_sem=send_main.at[(dx + 1) // 2],
            recv_sem=recv_main.at[(1 - dx) // 2],
            device_id=(gx + dx, gy),
            device_id_type=MESH,
        )

    def rim_copy(k, dx, dy):
        return pltpu.make_async_remote_copy(
            src_ref=send.at[span_x],
            dst_ref=landing(-dx, -dy),
            send_sem=send_rim.at[k],
            recv_sem=recv_rim.at[len(others) - 1 - k],
            device_id=(gx + dx, gy + dy),
            device_id_type=MESH,
        )

    def main_arrival(dx):
        return pltpu.make_async_remote_copy(
            src_ref=send.at[pl.ds(0, W)],
            dst_ref=from_x.at[(dx + 1) // 2, pl.ds(0, W)],
            send_sem=send_main.at[(dx + 1) // 2],
            recv_sem=recv_main.at[(dx + 1) // 2],
            device_id=(gx + dx, gy),
            device_id_type=MESH,
        )

    def rim_arrival(k, dx, dy):
        return pltpu.make_async_remote_copy(
            src_ref=send.at[span_x],
            dst_ref=landing(dx, dy),
            send_sem=send_rim.at[k],
            recv_sem=recv_rim.at[k],
            device_id=(gx + dx, gy + dy),
            device_id_type=MESH,
        )

    def masked(local_x, pairs, value):
        parts = []
        for pair in pairs:
            keep = jnp.broadcast_to(local_x // 2 == pair, (16, chunk))
            keep = jnp.where(keep, 1.0, 0.0).astype(BF)
            parts.append(value * jnp.concatenate([keep] * (2 * ROWS // 16), 0))
        return jnp.concatenate(parts, 0)

    def accumulate(total, left, right):
        total[...] += lax.dot_general(
            left, right, (((1,), (1,)), ((), ())), preferred_element_type=F32
        )

    def tile(pair, parity):
        at = (pair % (span_x // 4)) * 2 * ROWS
        cols = slice(parity * block_y, (parity + 1) * block_y)
        return acc[at : at + ROWS, cols] + acc[at + ROWS : at + 2 * ROWS, cols]

    def ready(first, last):
        for t in range(first, last):
            value = tile(t // 2, t % 2)
            if R <= t < R + block_x:
                value = value + jnp.where(inside, prior[t - R], 0.0)
            send[t] = value

    half = span_x // 4
    barrier = pltpu.get_barrier_semaphore()

    @pl.when(index == 0)
    def _():
        for dx, dy in others:
            @pl.when(present(dx, dy))
            def _():
                pl.semaphore_signal(
                    barrier, inc=1, device_id=(gx + dx, gy + dy), device_id_type=MESH
                )
        acc[...] = jnp.zeros_like(acc)
        acc_rim[...] = jnp.zeros_like(acc_rim)
        weighted[...] = jnp.zeros_like(weighted)
        prior[...] = jnp.zeros_like(prior)
        for x in range(block_x):
            prior[x, 0:species, :] = prior_weight * les[:, x, :]
            prior[x, species : species + 1, :] = jnp.full((1, block_y), prior_weight, F32)
            prior[x, species + 1 : species + 2, :] = 1.0 - jnp.exp(-rate[x : x + 1, :])
        for dx in (-1, 1):
            @pl.when(jnp.logical_not(has[dx][0]))
            def _():
                from_x[(dx + 1) // 2] = jnp.zeros((W + 1, ROWS, LANES), F32)
        for dx, dy in others:
            if dy != 0:
                @pl.when(jnp.logical_not(present(dx, dy)))
                def _():
                    landing(dx, dy)[...] = jnp.zeros((ROWS, LANES), F32)

    @pl.when(index < steps)
    def _():
        weighted[0:species, :] = comp[...] * mass[...]
        weighted[species : species + 1, :] = mass[...]
        value = weighted[...]
        high = value.astype(BF).astype(F32)
        both = jnp.concatenate([high, value - high], 0).astype(BF)
        split[index] = both
        local_x, inner, rim = positions(cell[...], block_x, block_y)
        column = jnp.where(inner < 0, -1, inner + (local_x % 2) * block_y)
        hot[index] = one_hot(column, 2 * block_y, 2 * block_y)
        hot_rim[...] = one_hot(rim, LANES, LANES)
        accumulate(acc, masked(local_x, range(half), both), hot[index])
        accumulate(acc_rim, both, hot_rim[...])

    @pl.when(index == steps - 1)
    def _():
        ready(0, W)
        rim_sum = acc_rim[0:ROWS, :] + acc_rim[ROWS:, :]
        for x in range(block_x):
            t = x + R
            low_at, high_at = t * W + R, side_size + t * W
            low, high = roll(prior[x], low_at), roll(prior[x], high_at + R)
            rim_sum += jnp.where((lane >= low_at) & (lane < low_at + R), low, 0.0)
            rim_sum += jnp.where((lane >= high_at) & (lane < high_at + R), high, 0.0)
        send[span_x] = rim_sum
        acc[...] = jnp.zeros_like(acc)
        number = (1 + (gx > 0).astype(jnp.int32) + (gx < counts[0] - 1).astype(jnp.int32)) * (
            1 + (gy > 0).astype(jnp.int32) + (gy < counts[1] - 1).astype(jnp.int32)
        ) - 1
        pl.semaphore_wait(barrier, number)

        @pl.when(has[-1][0])
        def _():
            main_copy(-1).start()

        for k, (dx, dy) in enumerate(others):
            @pl.when(present(dx, dy))
            def _():
                rim_copy(k, dx, dy).start()

    @pl.when(index >= steps)
    def _():
        at = index - steps
        local_x, _, _ = positions(cell[...], block_x, block_y)
        accumulate(acc, masked(local_x, range(half, 2 * half), split[at]), hot[at])

    @pl.when(index == 2 * steps - 1)
    def _():
        ready(W, span_x)

        @pl.when(has[1][0])
        def _():
            main_copy(1).start()

        for k, (dx, dy) in enumerate(others):
            @pl.when(present(dx, dy))
            def _():
                rim_arrival(k, dx, dy).wait_recv()

        @pl.when(has[1][0])
        def _():
            main_arrival(1).wait_recv()

        def finish(total, x):
            total_mass = total[species : species + 1, :]
            weight = jnp.where(total_mass > 0.0, total_mass, 1.0)
            weight = jnp.broadcast_to(weight, total.shape)
            value = total / jnp.where(row < species, weight, 1.0)
            table[x] = value
            return value

        low_side = lane < side_size
        place_x = jnp.where(low_side, lane, lane - side_size)
        used = lane < 2 * side_size
        behind = used & (place_x < 2 * R * W)
        ahead = used & (place_x >= block_x * W)
        total = send[span_x]
        for dx, dy in others:
            mask = used if dx == 0 else behind if dx < 0 else ahead
            if dy != 0:
                mask = mask & (low_side if dy < 0 else jnp.logical_not(low_side))
            shift = dx * block_x * W + dy * side_size
            total = total + jnp.where(mask, roll(landing(dx, dy)[...], shift), 0.0)
        rim_value = finish(total, span_x)

        def close(t):
            total = send[t]
            if t < W:
                total = total + from_x[0, t]
            if t >= block_x:
                total = total + from_x[1, t - block_x]
            value = finish(total, t)
            if R <= t < R + block_x:
                low_at, high_at = t * W + R, side_size + t * W
                value = jnp.where(lane < R, roll(rim_value, -low_at), value)
                value = jnp.where(
                    lane >= block_y - R, roll(rim_value, block_y - R - high_at), value
                )
                means[:, t - R, :] = value[0:species]

        for t in range(W, span_x):
            close(t)

        @pl.when(has[-1][0])
        def _():
            main_arrival(-1).wait_recv()

        for t in range(W):
            close(t)
        for k, (dx, dy) in enumerate(others):
            @pl.when(present(dx, dy))
            def _():
                rim_copy(k, dx, dy).wait_send()
        for dx in (-1, 1):
            @pl.when(has[dx][0])
            def _():
                main_copy(dx).wait_send()


def stack_levels(target, plain, matrices):
    species = matrices.shape[1]
    plain[...] = jnp.zeros_like(plain)
    plain[0:species, 0:species] = matrices[2]
    plain[HALF : HALF + NS_MID, 0:NS_MID] = matrices[1, 0:NS_MID, 0:NS_MID]
    base = HALF + NS_MID
    plain[base : base + NS_LOW, 0:NS_LOW] = matrices[0, 0:NS_LOW, 0:NS_LOW]
    high, low = halves(plain[...])
    target[:, 0:HALF] = high
    target[:, HALF : 2 * HALF] = high
    target[:, 2 * HALF :] = low


def react_kernel(
    block_x, block_y, comp, cell, level, table, rate, implicit, out,
    hot, hot_rim, left, left_rim, mixed, plain, left_rate, left_implicit,
):
    species = comp.shape[0]
    span_x = block_x + 2 * R

    @pl.when(pl.program_id(0) == 0)
    def _():
        mixed[...] = jnp.zeros_like(mixed)
        stack_levels(left_rate, plain, rate)
        stack_levels(left_implicit, plain, implicit)
        high, low = halves(table[0:span_x].reshape(span_x * ROWS, block_y))
        left[:, 0:block_y] = high
        left[:, block_y:] = low
        value = table[span_x]
        high = value.astype(BF).astype(F32)
        lane = lax.broadcasted_iota(jnp.int32, value.shape, 1)
        low = roll(value - high, LANES // 2)
        left_rim[0:ROWS, :] = jnp.where(lane < LANES // 2, high, low).astype(BF)

    local_x, inner, rim = positions(cell[...], block_x, block_y)
    once = one_hot(inner, block_y, block_y)
    hot[0:block_y, :] = once
    hot[block_y:, :] = once
    once = one_hot(rim, LANES // 2, LANES // 2)
    hot_rim[0 : LANES // 2, :] = once
    hot_rim[LANES // 2 :, :] = once
    rows = jnp.dot(left[...], hot[...], preferred_element_type=F32)
    taken = jnp.dot(left_rim[...], hot_rim[...], preferred_element_type=F32)
    taken = jnp.where(inner < 0, taken, 0.0)
    place = jnp.where(inner < 0, -1, local_x)
    for x in range(span_x):
        taken = jnp.where(place == x, rows[x * ROWS : (x + 1) * ROWS], taken)
    factor = taken[species + 1 : species + 2]
    comp_value = comp[...]
    mixed[0:species, :] = comp_value - factor * (comp_value - taken[0:species])
    levels = level[...]
    full, middle = levels == 2, levels == 1
    high, low = halves(mixed[...])
    right = jnp.concatenate([high, low, high], 0)
    drive = jnp.dot(left_rate[...], right, preferred_element_type=F32)
    base = HALF + NS_MID
    top = jnp.where(
        full, drive[0:NS_MID],
        jnp.where(middle, drive[HALF:base], drive[base : base + NS_MID]),
    )
    source = jnp.tanh(jnp.concatenate([top, drive[NS_MID:HALF]], 0))
    high, low = halves(source)
    right = jnp.concatenate([high, low, high], 0)
    change = jnp.dot(left_implicit[...], right, preferred_element_type=F32)
    top = jnp.where(
        full, change[0:NS_MID],
        jnp.where(middle, change[HALF:base], change[base : base + NS_MID]),
    )
    rest = jnp.where(full, change[NS_MID:species], 0.0)
    out[0:NS_MID, :] = mixed[0:NS_MID, :] + chem_step * top
    out[NS_MID:, :] = mixed[NS_MID:species, :] + chem_step * rest


def per_device(
    counts, composition, particle_mass, particle_cell, particle_level,
    les_mean, mix_rate, rate_matrix, implicit_map,
):
    species, particles = composition.shape
    block_x, block_y = les_mean.shape[1], les_mean.shape[2]
    span_x = block_x + 2 * R
    whole = pl.BlockSpec(memory_space=pltpu.VMEM)
    chunk = 2048
    steps = particles // chunk
    left_rows = span_x // 4 * 2 * ROWS

    def first_pass(rows):
        return pl.BlockSpec((rows, chunk), lambda i: (0, jnp.minimum(i, steps - 1)))

    dma = pltpu.SemaphoreType.DMA
    tiles = (span_x + 1, ROWS, LANES)
    table, means = pl.pallas_call(
        functools.partial(sums_kernel, counts, steps, chunk, block_x, block_y),
        grid=(2 * steps,),
        out_shape=(
            jax.ShapeDtypeStruct(tiles, F32),
            jax.ShapeDtypeStruct(les_mean.shape, F32),
        ),
        in_specs=[
            first_pass(species),
            first_pass(1),
            pl.BlockSpec((2, chunk), lambda i: (0, i % steps)),
            pl.BlockSpec(les_mean.shape, lambda i: (0, 0, 0)),
            pl.BlockSpec(mix_rate.shape, lambda i: (0, 0)),
        ],
        out_specs=(
            pl.BlockSpec(tiles, lambda i: (0, 0, 0)),
            pl.BlockSpec(les_mean.shape, lambda i: (0, 0, 0)),
        ),
        scratch_shapes=[
            pltpu.VMEM((steps, 2 * block_y, chunk), BF),
            pltpu.VMEM((LANES, chunk), BF),
            pltpu.VMEM((ROWS, chunk), F32),
            pltpu.VMEM((steps, 2 * ROWS, chunk), BF),
            pltpu.VMEM((left_rows, 2 * block_y), F32),
            pltpu.VMEM((2 * ROWS, LANES), F32),
            pltpu.VMEM(tiles, F32),
            pltpu.VMEM((block_x, ROWS, block_y), F32),
            pltpu.VMEM((2, W + 1, ROWS, LANES), F32),
            pltpu.VMEM((2, ROWS, LANES), F32),
            pltpu.VMEM((2, 2, ROWS, LANES), F32),
            dma((2,)), dma((2,)), dma((8,)), dma((8,)),
        ],
        compiler_params=pltpu.CompilerParams(
            collective_id=0, has_side_effects=True, vmem_limit_bytes=60 << 20
        ),
    )(composition, particle_mass[None], particle_cell, les_mean, mix_rate)
    stacked = HALF + 2 * NS_MID
    chunk = 1024

    def by_chunk(rows):
        return pl.BlockSpec((rows, chunk), lambda i: (0, i))

    updated = pl.pallas_call(
        functools.partial(react_kernel, block_x, block_y),
        grid=(particles // chunk,),
        out_shape=jax.ShapeDtypeStruct(composition.shape, F32),
        in_specs=[by_chunk(species), by_chunk(2), by_chunk(1), whole, whole, whole],
        out_specs=by_chunk(species),
        scratch_shapes=[
            pltpu.VMEM((2 * block_y, chunk), BF),
            pltpu.VMEM((LANES, chunk), BF),
            pltpu.VMEM((span_x * ROWS, 2 * block_y), BF),
            pltpu.VMEM((ROWS, LANES), BF),
            pltpu.VMEM((HALF, chunk), F32),
            pltpu.VMEM((stacked, HALF), F32),
            pltpu.VMEM((stacked, 3 * HALF), BF),
            pltpu.VMEM((stacked, 3 * HALF), BF),
        ],
        compiler_params=pltpu.CompilerParams(vmem_limit_bytes=48 << 20),
    )(composition, particle_cell, particle_level[None], table, rate_matrix, implicit_map)
    return updated, means


def solution(mesh):
    placed = (
        P(None, ("gx", "gy")),
        P(("gx", "gy")),
        P(None, ("gx", "gy")),
        P(("gx", "gy")),
        P(None, "gx", "gy"),
        P("gx", "gy"),
        P(),
        P(),
    )
    return jax.shard_map(
        functools.partial(per_device, (mesh.shape["gx"], mesh.shape["gy"])),
        mesh=mesh,
        in_specs=placed,
        out_specs=(P(None, ("gx", "gy")), P(None, "gx", "gy")),
        check_vma=False,
    )
```

time: 34.6 us -> 25.3 us (0.73)
  the two profiles are of different devices: /device:TPU:19 before, /device:TPU:1 now
where the time goes in v2:
time: 25.3 us; the launch traced here: 24.9 us
  Pallas kernels  21.7 us (86%)
  local copies, waits for them, and re-layouts  2.49 us (10%)
  between operations  0.71 us (3%)
    pallas_call x1, Pallas kernels, per_device(): pl.pallas_call(functools.partial(sums_kernel, counts, steps, chunk, block...  12.8 us
    pallas_call x1, Pallas kernels, per_device(): pl.pallas_call(functools.partial(react_kernel, block_x, block_y), grid=(p...  8.97 us
    unnamed x15, local copies, waits for them, and re-layouts  2.49 us

profile of v2, /device:TPU:1, one launch (start us, length us, event | category | flops | bytes accessed | tf_op | source)
XLA Modules:
  0.0 24.9 jit_solution(5834171558012840796)
XLA Ops:
  0.6 0.0 copy-start.1
  0.6 0.0 copy-start
  0.7 0.0 copy-start.3
  0.7 0.0 copy-start.5
  0.7 12.8 %shard_map.95 = (f32[9,56,128]{2,1,0:T(8,128)}, f32[53,4,128]{2,1,0:T(4,128)}) custom-call(f32[53,8192]{1,0:T(8,128)} %comp.3, f32[1,8192]{1,0:T(1,128)} %bitcast.3, s32[2,8192]{1,0:T(2,128)} %cell.3, f32[53,4,128]{2,1,0:T(4,128)} %les.1, f32[4,128]{1,0:T(4,128)} %rate.2), custom_call_target="tpu_custom_call" | custom-call | tf_op jit(solution)/shard_map/pallas_call | solution.py:385
  13.4 0.0 copy-done.1
  13.5 0.0 copy-done
  13.5 0.0 copy-done.3
  13.5 0.0 copy-done.5
  13.5 0.0 copy-start.2
  13.5 0.9 %copy-done.2 = f32[9,56,128]{2,1,0:T(8,128)S(1)} copy-done((f32[9,56,128]{2,1,0:T(8,128)S(1)}, f32[9,56,128]{2,1,0:T(8,128)}, u32[]{:S(2)}) %copy-start.2) | copy-done | bytes 258072
  14.4 0.0 copy-start.4
  14.4 0.9 %copy-done.4 = f32[3,53,53]{2,1,0:T(8,128)S(1)} copy-done((f32[3,53,53]{2,1,0:T(8,128)S(1)}, f32[3,53,53]{2,1,0:T(8,128)}, u32[]{:S(2)}) %copy-start.4) | copy-done | bytes 33732
  15.3 0.0 copy-start.6
  15.3 9.0 %shard_map.96 = f32[53,8192]{1,0:T(8,128)} custom-call(f32[53,8192]{1,0:T(8,128)S(1)} %copy-done, s32[2,8192]{1,0:T(2,128)S(1)} %copy-done.1, s32[1,8192]{1,0:T(1,128)S(1)} %bitcast.2, f32[9,56,128]{2,1,0:T(8,128)S(1)} %copy-done.2, f32[3,53,53]{2,1,0:T(8,128)S(1)} %copy-done.3, f32[3,53,53]{2,1,0:T(8,128)S(1)} %copy-done.4), custom_call_target="tpu_custom_call" | custom-call | tf_op jit(solution)/shard_map/pallas_call | solution.py:427
  24.3 0.0 copy-done.6
  24.3 0.6 %copy.11 = f32[53,4,128]{2,1,0:T(4,128)} copy(f32[53,4,128]{2,1,0:T(4,128)S(1)} %copy-done.6) | data formatting | bytes 217088
Async XLA Ops:
  0.6 12.8 %copy-start.1 = (s32[2,8192]{1,0:T(2,128)S(1)}, s32[2,8192]{1,0:T(2,128)}, u32[]{:S(2)}) copy-start(s32[2,8192]{1,0:T(2,128)} %cell.3) | copy-start | bytes 196612
  0.6 12.8 %copy-start = (f32[53,8192]{1,0:T(8,128)S(1)}, f32[53,8192]{1,0:T(8,128)}, u32[]{:S(2)}) copy-start(f32[53,8192]{1,0:T(8,128)} %comp.3) | copy-start | bytes 5210116
  0.7 12.8 %copy-start.3 = (f32[3,53,53]{2,1,0:T(8,128)S(1)}, f32[3,53,53]{2,1,0:T(8,128)}, u32[]{:S(2)}) copy-start(f32[3,53,53]{2,1,0:T(8,128)} %rate.3) | copy-start | bytes 101128
  0.7 12.8 %copy-start.5 = (s32[8192]{0:T(1024)S(1)}, s32[8192]{0:T(1024)}, u32[]{:S(2)}) copy-start(s32[8192]{0:T(1024)} %param.11) | copy-start | bytes 98308
  13.5 0.9 %copy-start.2 = (f32[9,56,128]{2,1,0:T(8,128)S(1)}, f32[9,56,128]{2,1,0:T(8,128)}, u32[]{:S(2)}) copy-start(f32[9,56,128]{2,1,0:T(8,128)} %get-tuple-element.4.table) | copy-start | bytes 774148
  14.4 0.9 %copy-start.4 = (f32[3,53,53]{2,1,0:T(8,128)S(1)}, f32[3,53,53]{2,1,0:T(8,128)}, u32[]{:S(2)}) copy-start(f32[3,53,53]{2,1,0:T(8,128)} %implicit.1) | copy-start | bytes 101128
  15.3 9.0 %copy-start.6 = (f32[53,4,128]{2,1,0:T(4,128)S(1)}, f32[53,4,128]{2,1,0:T(4,128)}, u32[]{:S(2)}) copy-start(f32[53,4,128]{2,1,0:T(4,128)} %get-tuple-element.9) | copy-start | bytes 325636

commit v3 on v2

--- a/solution.py
+++ b/solution.py
@@ -40,15 +40,16 @@
     return local_x, jnp.where(on_rim, -1, local_y - R), jnp.where(on_rim, rim, -1)
 
 
-def one_hot(place, rows, period):
+def one_hot(place, rows):
     sub = lax.broadcasted_iota(jnp.int32, (rows, place.shape[1]), 0)
-    if period < rows:
-        sub = sub % period
-    return jnp.where(sub == place, 1.0, 0.0).astype(BF)
+    same = sub.astype(F32).astype(BF) == jnp.broadcast_to(
+        place.astype(F32), (rows, place.shape[1])
+    ).astype(BF)
+    return jnp.where(same, jnp.ones((), BF), jnp.zeros((), BF))
 
 
 def sums_kernel(
-    counts, steps, chunk, block_x, block_y, comp, mass, cell, les, rate, table, means,
+    counts, steps, chunk, block_x, block_y, comp, mass, cell, les, rate, table,
     hot, hot_rim, weighted, split, acc, acc_rim,
     send, prior, from_x, from_y, from_xy, send_main, recv_main, send_rim, recv_rim,
 ):
@@ -182,10 +183,12 @@
         split[index] = both
         local_x, inner, rim = positions(cell[...], block_x, block_y)
         column = jnp.where(inner < 0, -1, inner + (local_x % 2) * block_y)
-        hot[index] = one_hot(column, 2 * block_y, 2 * block_y)
-        hot_rim[...] = one_hot(rim, LANES, LANES)
+        hot[index] = one_hot(column, 2 * block_y)
+        hot_rim[...] = one_hot(rim, HALF)
         accumulate(acc, masked(local_x, range(half), both), hot[index])
-        accumulate(acc_rim, both, hot_rim[...])
+        acc_rim[:, 0:HALF] += lax.dot_general(
+            both, hot_rim[...], (((1,), (1,)), ((), ())), preferred_element_type=F32
+        )
 
     @pl.when(index == steps - 1)
     def _():
@@ -236,13 +239,11 @@
         def _():
             main_arrival(1).wait_recv()
 
-        def finish(total, x):
+        def finish(total):
             total_mass = total[species : species + 1, :]
             weight = jnp.where(total_mass > 0.0, total_mass, 1.0)
             weight = jnp.broadcast_to(weight, total.shape)
-            value = total / jnp.where(row < species, weight, 1.0)
-            table[x] = value
-            return value
+            return total / jnp.where(row < species, weight, 1.0)
 
         low_side = lane < side_size
         place_x = jnp.where(low_side, lane, lane - side_size)
@@ -256,7 +257,8 @@
                 mask = mask & (low_side if dy < 0 else jnp.logical_not(low_side))
             shift = dx * block_x * W + dy * side_size
             total = total + jnp.where(mask, roll(landing(dx, dy)[...], shift), 0.0)
-        rim_value = finish(total, span_x)
+        rim_value = finish(total)
+        table[span_x] = rim_value
 
         def close(t):
             total = send[t]
@@ -264,14 +266,14 @@
                 total = total + from_x[0, t]
             if t >= block_x:
                 total = total + from_x[1, t - block_x]
-            value = finish(total, t)
+            value = finish(total)
             if R <= t < R + block_x:
                 low_at, high_at = t * W + R, side_size + t * W
                 value = jnp.where(lane < R, roll(rim_value, -low_at), value)
                 value = jnp.where(
                     lane >= block_y - R, roll(rim_value, block_y - R - high_at), value
                 )
-                means[:, t - R, :] = value[0:species]
+            table[t] = value
 
         for t in range(W, span_x):
             close(t)
@@ -306,11 +308,12 @@
 
 
 def react_kernel(
-    block_x, block_y, comp, cell, level, table, rate, implicit, out,
-    hot, hot_rim, left, left_rim, mixed, plain, left_rate, left_implicit,
+    block_x, block_y, comp, cell, level, table, rate, implicit, out, means,
+    left, left_rim, mixed, plain, left_rate, left_implicit,
 ):
     species = comp.shape[0]
     span_x = block_x + 2 * R
+    piece = 256
 
     @pl.when(pl.program_id(0) == 0)
     def _():
@@ -323,46 +326,62 @@
         value = table[span_x]
         high = value.astype(BF).astype(F32)
         lane = lax.broadcasted_iota(jnp.int32, value.shape, 1)
-        low = roll(value - high, LANES // 2)
-        left_rim[0:ROWS, :] = jnp.where(lane < LANES // 2, high, low).astype(BF)
-
-    local_x, inner, rim = positions(cell[...], block_x, block_y)
-    once = one_hot(inner, block_y, block_y)
-    hot[0:block_y, :] = once
-    hot[block_y:, :] = once
-    once = one_hot(rim, LANES // 2, LANES // 2)
-    hot_rim[0 : LANES // 2, :] = once
-    hot_rim[LANES // 2 :, :] = once
-    rows = jnp.dot(left[...], hot[...], preferred_element_type=F32)
-    taken = jnp.dot(left_rim[...], hot_rim[...], preferred_element_type=F32)
-    taken = jnp.where(inner < 0, taken, 0.0)
-    place = jnp.where(inner < 0, -1, local_x)
-    for x in range(span_x):
-        taken = jnp.where(place == x, rows[x * ROWS : (x + 1) * ROWS], taken)
-    factor = taken[species + 1 : species + 2]
-    comp_value = comp[...]
-    mixed[0:species, :] = comp_value - factor * (comp_value - taken[0:species])
-    levels = level[...]
-    full, middle = levels == 2, levels == 1
-    high, low = halves(mixed[...])
-    right = jnp.concatenate([high, low, high], 0)
-    drive = jnp.dot(left_rate[...], right, preferred_element_type=F32)
-    base = HALF + NS_MID
-    top = jnp.where(
-        full, drive[0:NS_MID],
-        jnp.where(middle, drive[HALF:base], drive[base : base + NS_MID]),
-    )
-    source = jnp.tanh(jnp.concatenate([top, drive[NS_MID:HALF]], 0))
-    high, low = halves(source)
-    right = jnp.concatenate([high, low, high], 0)
-    change = jnp.dot(left_implicit[...], right, preferred_element_type=F32)
-    top = jnp.where(
-        full, change[0:NS_MID],
-        jnp.where(middle, change[HALF:base], change[base : base + NS_MID]),
-    )
-    rest = jnp.where(full, change[NS_MID:species], 0.0)
-    out[0:NS_MID, :] = mixed[0:NS_MID, :] + chem_step * top
-    out[NS_MID:, :] = mixed[NS_MID:species, :] + chem_step * rest
+        low = roll(value - high, HALF)
+        left_rim[...] = jnp.where(lane < HALF, high, low).astype(BF)
+        for x in range(block_x):
+            means[:, x, :] = table[x + R, 0:species, :]
+
+    def choose(test, yes, no):
+        shape = (yes.shape[0] // 8, 8, piece)
+        return jnp.where(test[None], yes.reshape(shape), no.reshape(shape)).reshape(yes.shape)
+
+    def work(at):
+        span = slice(at, at + piece)
+        local_x, inner, rim = positions(cell[:, span], block_x, block_y)
+        hot = one_hot(inner, block_y)
+        hot_rim = one_hot(rim, HALF)
+        rows = jnp.dot(left[...], jnp.concatenate([hot, hot], 0), preferred_element_type=F32)
+        on_rim = jnp.dot(
+            left_rim[...], jnp.concatenate([hot_rim, hot_rim], 0), preferred_element_type=F32
+        )
+        place = jnp.broadcast_to(local_x, (8, piece))
+        parts = [rows[x * ROWS : (x + 1) * ROWS] for x in range(span_x)]
+        bit = 1
+        while len(parts) > 1:
+            test = (place & bit) != 0
+            paired = [
+                choose(test, parts[i + 1], parts[i]) for i in range(0, len(parts) - 1, 2)
+            ]
+            parts = paired + parts[2 * len(paired) :]
+            bit *= 2
+        taken = choose(jnp.broadcast_to(inner, (8, piece)) < 0, on_rim, parts[0])
+        factor = taken[species + 1 : species + 2]
+        comp_value = comp[:, span]
+        mixed[0:species, span] = comp_value - factor * (comp_value - taken[0:species])
+        levels = jnp.broadcast_to(level[:, span], (8, piece))
+        full, middle = levels == 2, levels == 1
+        base = HALF + NS_MID
+
+        def pick(value):
+            return choose(
+                full, value[0:NS_MID],
+                choose(middle, value[HALF:base], value[base : base + NS_MID]),
+            )
+
+        high, low = halves(mixed[:, span])
+        right = jnp.concatenate([high, low, high], 0)
+        drive = jnp.dot(left_rate[...], right, preferred_element_type=F32)
+        source = jnp.tanh(jnp.concatenate([pick(drive), drive[NS_MID:HALF]], 0))
+        high, low = halves(source)
+        right = jnp.concatenate([high, low, high], 0)
+        change = jnp.dot(left_implicit[...], right, preferred_element_type=F32)
+        rest = change[NS_MID:ROWS]
+        rest = choose(full, rest, jnp.zeros_like(rest))
+        out[0:NS_MID, span] = mixed[0:NS_MID, span] + chem_step * pick(change)
+        out[NS_MID:, span] = mixed[NS_MID:species, span] + chem_step * rest[0 : species - NS_MID]
+
+    for at in range(0, comp.shape[1], piece):
+        work(at)
 
 
 def per_device(
@@ -382,13 +401,10 @@
 
     dma = pltpu.SemaphoreType.DMA
     tiles = (span_x + 1, ROWS, LANES)
-    table, means = pl.pallas_call(
+    table = pl.pallas_call(
         functools.partial(sums_kernel, counts, steps, chunk, block_x, block_y),
         grid=(2 * steps,),
-        out_shape=(
-            jax.ShapeDtypeStruct(tiles, F32),
-            jax.ShapeDtypeStruct(les_mean.shape, F32),
-        ),
+        out_shape=jax.ShapeDtypeStruct(tiles, F32),
         in_specs=[
             first_pass(species),
             first_pass(1),
@@ -396,13 +412,10 @@
             pl.BlockSpec(les_mean.shape, lambda i: (0, 0, 0)),
             pl.BlockSpec(mix_rate.shape, lambda i: (0, 0)),
         ],
-        out_specs=(
-            pl.BlockSpec(tiles, lambda i: (0, 0, 0)),
-            pl.BlockSpec(les_mean.shape, lambda i: (0, 0, 0)),
-        ),
+        out_specs=pl.BlockSpec(tiles, lambda i: (0, 0, 0)),
         scratch_shapes=[
             pltpu.VMEM((steps, 2 * block_y, chunk), BF),
-            pltpu.VMEM((LANES, chunk), BF),
+            pltpu.VMEM((HALF, chunk), BF),
             pltpu.VMEM((ROWS, chunk), F32),
             pltpu.VMEM((steps, 2 * ROWS, chunk), BF),
             pltpu.VMEM((left_rows, 2 * block_y), F32),
@@ -424,15 +437,22 @@
     def by_chunk(rows):
         return pl.BlockSpec((rows, chunk), lambda i: (0, i))
 
-    updated = pl.pallas_call(
+    def fixed(array):
+        return pl.BlockSpec(array.shape, lambda i: (0,) * array.ndim)
+
+    return pl.pallas_call(
         functools.partial(react_kernel, block_x, block_y),
         grid=(particles // chunk,),
-        out_shape=jax.ShapeDtypeStruct(composition.shape, F32),
-        in_specs=[by_chunk(species), by_chunk(2), by_chunk(1), whole, whole, whole],
-        out_specs=by_chunk(species),
+        out_shape=(
+            jax.ShapeDtypeStruct(composition.shape, F32),
+            jax.ShapeDtypeStruct(les_mean.shape, F32),
+        ),
+        in_specs=[
+            by_chunk(species), by_chunk(2), by_chunk(1),
+            fixed(table), fixed(rate_matrix), fixed(implicit_map),
+        ],
+        out_specs=(by_chunk(species), fixed(les_mean)),
         scratch_shapes=[
-            pltpu.VMEM((2 * block_y, chunk), BF),
-            pltpu.VMEM((LANES, chunk), BF),
             pltpu.VMEM((span_x * ROWS, 2 * block_y), BF),
             pltpu.VMEM((ROWS, LANES), BF),
             pltpu.VMEM((HALF, chunk), F32),
@@ -440,9 +460,8 @@
             pltpu.VMEM((stacked, 3 * HALF), BF),
             pltpu.VMEM((stacked, 3 * HALF), BF),
         ],
-        compiler_params=pltpu.CompilerParams(vmem_limit_bytes=48 << 20),
+        compiler_params=pltpu.CompilerParams(vmem_limit_bytes=60 << 20),
     )(composition, particle_cell, particle_level[None], table, rate_matrix, implicit_map)
-    return updated, means
 
 
 def solution(mesh):

time: 25.3 us -> 31.4 us (1.24)
  Pallas kernels: 21.7 us -> 30.4 us
  local copies, waits for them, and re-layouts: 2.49 us -> 0 us
    pallas_call x1, Pallas kernels: 8.97 us -> 18.2 us  [per_device(): pl.pallas_call(functools.partial(react_kernel, block_x, block_y), grid=(p...]
    unnamed x15 -> x0, local copies, waits for them, and re-layouts: 2.49 us -> none
    pallas_call x1, Pallas kernels: 12.8 us -> 12.2 us  [per_device(): pl.pallas_call(functools.partial(sums_kernel, counts, steps, chunk, block...]
where the time goes in v3:
time: 31.4 us; the launch traced here: 31 us
  Pallas kernels  30.4 us (97%)
  between operations  0.64 us (2%)
    pallas_call x1, Pallas kernels, per_device(): pl.pallas_call(functools.partial(react_kernel, block_x, block_y), grid=(p...  18.2 us
    pallas_call x1, Pallas kernels, per_device(): pl.pallas_call(functools.partial(sums_kernel, counts, steps, chunk, block...  12.2 us

profile of v3, /device:TPU:1, one launch (start us, length us, event | category | flops | bytes accessed | tf_op | source)
XLA Modules:
  0.0 31.0 jit_solution(16386210935010984847)
XLA Ops:
  0.6 12.2 %shard_map.95.table = f32[9,56,128]{2,1,0:T(8,128)} custom-call(f32[53,8192]{1,0:T(8,128)} %comp.3, f32[1,8192]{1,0:T(1,128)} %bitcast.2, s32[2,8192]{1,0:T(2,128)} %cell.3, f32[53,4,128]{2,1,0:T(4,128)} %les.1, f32[4,128]{1,0:T(4,128)} %rate.2), custom_call_target="tpu_custom_call" | custom-call | tf_op jit(solution)/shard_map/pallas_call | solution.py:404
  12.8 18.2 %shard_map.96 = (f32[53,8192]{1,0:T(8,128)}, f32[53,4,128]{2,1,0:T(4,128)}) custom-call(f32[53,8192]{1,0:T(8,128)} %comp.3, s32[2,8192]{1,0:T(2,128)} %cell.3, s32[1,8192]{1,0:T(1,128)} %bitcast.3, f32[9,56,128]{2,1,0:T(8,128)} %shard_map.95.table, f32[3,53,53]{2,1,0:T(8,128)} %rate.3, f32[3,53,53]{2,1,0:T(8,128)} %implicit.1), custom_call_target="tpu_custom_call" | custom-call | tf_op jit(solution)/shard_map/pallas_call | solution.py:443

commit v4 on v3

--- a/solution.py
+++ b/solution.py
@@ -313,7 +313,7 @@
 ):
     species = comp.shape[0]
     span_x = block_x + 2 * R
-    piece = 256
+    piece = 2048
 
     @pl.when(pl.program_id(0) == 0)
     def _():
@@ -432,7 +432,7 @@
         ),
     )(composition, particle_mass[None], particle_cell, les_mean, mix_rate)
     stacked = HALF + 2 * NS_MID
-    chunk = 1024
+    chunk = 2048
 
     def by_chunk(rows):
         return pl.BlockSpec((rows, chunk), lambda i: (0, i))

time: 31.4 us -> 20.6 us (0.66)
  Pallas kernels: 30.4 us -> 19.6 us
    pallas_call x1, Pallas kernels: 18.2 us -> 7.44 us  [per_device(): pl.pallas_call(functools.partial(react_kernel, block_x, block_y), grid=(p...]
where the time goes in v4:
time: 20.6 us; the launch traced here: 20.3 us
  Pallas kernels  19.6 us (95%)
  between operations  0.64 us (3%)
    pallas_call x1, Pallas kernels, per_device(): pl.pallas_call(functools.partial(sums_kernel, counts, steps, chunk, block...  12.2 us
    pallas_call x1, Pallas kernels, per_device(): pl.pallas_call(functools.partial(react_kernel, block_x, block_y), grid=(p...  7.44 us

profile of v4, /device:TPU:1, one launch (start us, length us, event | category | flops | bytes accessed | tf_op | source)
XLA Modules:
  0.0 20.3 jit_solution(15415796143795302276)
XLA Ops:
  0.6 12.2 %shard_map.95.table = f32[9,56,128]{2,1,0:T(8,128)} custom-call(f32[53,8192]{1,0:T(8,128)} %comp.3, f32[1,8192]{1,0:T(1,128)} %bitcast.2, s32[2,8192]{1,0:T(2,128)} %cell.3, f32[53,4,128]{2,1,0:T(4,128)} %les.1, f32[4,128]{1,0:T(4,128)} %rate.2), custom_call_target="tpu_custom_call" | custom-call | tf_op jit(solution)/shard_map/pallas_call | solution.py:404
  12.8 7.4 %shard_map.96 = (f32[53,8192]{1,0:T(8,128)}, f32[53,4,128]{2,1,0:T(4,128)}) custom-call(f32[53,8192]{1,0:T(8,128)} %comp.3, s32[2,8192]{1,0:T(2,128)} %cell.3, s32[1,8192]{1,0:T(1,128)} %bitcast.3, f32[9,56,128]{2,1,0:T(8,128)} %shard_map.95.table, f32[3,53,53]{2,1,0:T(8,128)} %rate.3, f32[3,53,53]{2,1,0:T(8,128)} %implicit.1), custom_call_target="tpu_custom_call" | custom-call | tf_op jit(solution)/shard_map/pallas_call | solution.py:443

commit v5 on v4

--- a/solution.py
+++ b/solution.py
@@ -460,7 +460,7 @@
             pltpu.VMEM((stacked, 3 * HALF), BF),
             pltpu.VMEM((stacked, 3 * HALF), BF),
         ],
-        compiler_params=pltpu.CompilerParams(vmem_limit_bytes=60 << 20),
+        compiler_params=pltpu.CompilerParams(vmem_limit_bytes=40 << 20),
     )(composition, particle_cell, particle_level[None], table, rate_matrix, implicit_map)
 
 

time: 20.6 us -> 20.6 us (level)
  Pallas kernels: 19.6 us -> 18.6 us
  local copies, waits for them, and re-layouts: 0 us -> 0.96 us
    pallas_call x1, Pallas kernels: 7.44 us -> 6.28 us  [per_device(): pl.pallas_call(functools.partial(react_kernel, block_x, block_y), grid=(p...]
    unnamed x0 -> x12, local copies, waits for them, and re-layouts: none -> 0.96 us
where the time goes in v5:
time: 20.6 us; the launch traced here: 20.3 us
  Pallas kernels  18.6 us (90%)
  local copies, waits for them, and re-layouts  0.96 us (5%)
  between operations  0.73 us (4%)
    pallas_call x1, Pallas kernels, per_device(): pl.pallas_call(functools.partial(sums_kernel, counts, steps, chunk, block...  12.3 us
    pallas_call x1, Pallas kernels, per_device(): pl.pallas_call(functools.partial(react_kernel, block_x, block_y), grid=(p...  6.28 us
    unnamed x12, local copies, waits for them, and re-layouts  0.96 us

profile of v5, /device:TPU:1, one launch (start us, length us, event | category | flops | bytes accessed | tf_op | source)
XLA Modules:
  0.0 20.3 jit_solution(6978466430602722482)
XLA Ops:
  0.6 0.0 copy-start.2
  0.6 0.0 copy-start
  0.7 0.0 copy-start.4
  0.7 0.0 copy-start.3
  0.7 0.0 copy-start.5
  0.7 12.3 %shard_map.95.table = f32[9,56,128]{2,1,0:T(8,128)} custom-call(f32[53,8192]{1,0:T(8,128)} %comp.3, f32[1,8192]{1,0:T(1,128)} %bitcast.3, s32[2,8192]{1,0:T(2,128)} %cell.3, f32[53,4,128]{2,1,0:T(4,128)} %les.1, f32[4,128]{1,0:T(4,128)} %rate.2), custom_call_target="tpu_custom_call" | custom-call | tf_op jit(solution)/shard_map/pallas_call | solution.py:404
  13.0 0.0 copy-done.2
  13.0 0.0 copy-done
  13.0 0.0 copy-done.4
  13.0 0.0 copy-done.3
  13.0 0.0 copy-done.5
  13.0 0.0 copy-start.1
  13.1 0.9 %copy-done.1 = f32[9,56,128]{2,1,0:T(8,128)S(1)} copy-done((f32[9,56,128]{2,1,0:T(8,128)S(1)}, f32[9,56,128]{2,1,0:T(8,128)}, u32[]{:S(2)}) %copy-start.1) | copy-done | bytes 258072
  14.0 6.3 %shard_map.96 = (f32[53,8192]{1,0:T(8,128)}, f32[53,4,128]{2,1,0:T(4,128)}) custom-call(f32[53,8192]{1,0:T(8,128)S(1)} %copy-done, s32[2,8192]{1,0:T(2,128)S(1)} %copy-done.2, s32[1,8192]{1,0:T(1,128)S(1)} %bitcast.2, f32[9,56,128]{2,1,0:T(8,128)S(1)} %copy-done.1, f32[3,53,53]{2,1,0:T(8,128)S(1)} %copy-done.3, f32[3,53,53]{2,1,0:T(8,128)S(1)} %copy-done.4), custom_call_target="tpu_custom_call" | custom-call | tf_op jit(solution)/shard_map/pallas_call | solution.py:443
Async XLA Ops:
  0.6 12.4 %copy-start.2 = (s32[2,8192]{1,0:T(2,128)S(1)}, s32[2,8192]{1,0:T(2,128)}, u32[]{:S(2)}) copy-start(s32[2,8192]{1,0:T(2,128)} %cell.3) | copy-start | bytes 196612
  0.6 12.4 %copy-start = (f32[53,8192]{1,0:T(8,128)S(1)}, f32[53,8192]{1,0:T(8,128)}, u32[]{:S(2)}) copy-start(f32[53,8192]{1,0:T(8,128)} %comp.3) | copy-start | bytes 5210116
  0.7 12.4 %copy-start.4 = (f32[3,53,53]{2,1,0:T(8,128)S(1)}, f32[3,53,53]{2,1,0:T(8,128)}, u32[]{:S(2)}) copy-start(f32[3,53,53]{2,1,0:T(8,128)} %implicit.1) | copy-start | bytes 101128
  0.7 12.4 %copy-start.3 = (f32[3,53,53]{2,1,0:T(8,128)S(1)}, f32[3,53,53]{2,1,0:T(8,128)}, u32[]{:S(2)}) copy-start(f32[3,53,53]{2,1,0:T(8,128)} %rate.3) | copy-start | bytes 101128
  0.7 12.4 %copy-start.5 = (s32[8192]{0:T(1024)S(1)}, s32[8192]{0:T(1024)}, u32[]{:S(2)}) copy-start(s32[8192]{0:T(1024)} %param.11) | copy-start | bytes 98308
  13.0 0.9 %copy-start.1 = (f32[9,56,128]{2,1,0:T(8,128)S(1)}, f32[9,56,128]{2,1,0:T(8,128)}, u32[]{:S(2)}) copy-start(f32[9,56,128]{2,1,0:T(8,128)} %shard_map.95.table) | copy-start | bytes 774148

commit v6 on v5

--- a/solution.py
+++ b/solution.py
@@ -392,7 +392,7 @@
     block_x, block_y = les_mean.shape[1], les_mean.shape[2]
     span_x = block_x + 2 * R
     whole = pl.BlockSpec(memory_space=pltpu.VMEM)
-    chunk = 2048
+    chunk = 4096
     steps = particles // chunk
     left_rows = span_x // 4 * 2 * ROWS
 

time: 20.6 us -> 20.2 us (0.981)
  the two profiles are of different devices: /device:TPU:1 before, /device:TPU:19 now
where the time goes in v6:
time: 20.2 us; the launch traced here: 20.1 us
  Pallas kernels  18.4 us (91%)
  local copies, waits for them, and re-layouts  0.96 us (5%)
  between operations  0.73 us (4%)
    pallas_call x1, Pallas kernels, per_device(): pl.pallas_call(functools.partial(sums_kernel, counts, steps, chunk, block...  12.1 us
    pallas_call x1, Pallas kernels, per_device(): pl.pallas_call(functools.partial(react_kernel, block_x, block_y), grid=(p...  6.27 us
    unnamed x12, local copies, waits for them, and re-layouts  0.96 us

profile of v6, /device:TPU:19, one launch (start us, length us, event | category | flops | bytes accessed | tf_op | source)
XLA Modules:
  0.0 20.1 jit_solution(6673592032829468436)
XLA Ops:
  0.6 0.0 copy-start.2
  0.6 0.0 copy-start
  0.7 0.0 copy-start.4
  0.7 0.0 copy-start.3
  0.7 0.0 copy-start.5
  0.7 12.1 %shard_map.95.table = f32[9,56,128]{2,1,0:T(8,128)} custom-call(f32[53,8192]{1,0:T(8,128)} %comp.3, f32[1,8192]{1,0:T(1,128)} %bitcast.3, s32[2,8192]{1,0:T(2,128)} %cell.3, f32[53,4,128]{2,1,0:T(4,128)} %les.1, f32[4,128]{1,0:T(4,128)} %rate.2), custom_call_target="tpu_custom_call" | custom-call | tf_op jit(solution)/shard_map/pallas_call | solution.py:404
  12.8 0.0 copy-done.2
  12.8 0.0 copy-done
  12.8 0.0 copy-done.4
  12.8 0.0 copy-done.3
  12.8 0.0 copy-done.5
  12.9 0.0 copy-start.1
  12.9 0.9 %copy-done.1 = f32[9,56,128]{2,1,0:T(8,128)S(1)} copy-done((f32[9,56,128]{2,1,0:T(8,128)S(1)}, f32[9,56,128]{2,1,0:T(8,128)}, u32[]{:S(2)}) %copy-start.1) | copy-done | bytes 258072
  13.8 6.3 %shard_map.96 = (f32[53,8192]{1,0:T(8,128)}, f32[53,4,128]{2,1,0:T(4,128)}) custom-call(f32[53,8192]{1,0:T(8,128)S(1)} %copy-done, s32[2,8192]{1,0:T(2,128)S(1)} %copy-done.2, s32[1,8192]{1,0:T(1,128)S(1)} %bitcast.2, f32[9,56,128]{2,1,0:T(8,128)S(1)} %copy-done.1, f32[3,53,53]{2,1,0:T(8,128)S(1)} %copy-done.3, f32[3,53,53]{2,1,0:T(8,128)S(1)} %copy-done.4), custom_call_target="tpu_custom_call" | custom-call | tf_op jit(solution)/shard_map/pallas_call | solution.py:443
Async XLA Ops:
  0.6 12.2 %copy-start.2 = (s32[2,8192]{1,0:T(2,128)S(1)}, s32[2,8192]{1,0:T(2,128)}, u32[]{:S(2)}) copy-start(s32[2,8192]{1,0:T(2,128)} %cell.3) | copy-start | bytes 196612
  0.6 12.2 %copy-start = (f32[53,8192]{1,0:T(8,128)S(1)}, f32[53,8192]{1,0:T(8,128)}, u32[]{:S(2)}) copy-start(f32[53,8192]{1,0:T(8,128)} %comp.3) | copy-start | bytes 5210116
  0.7 12.2 %copy-start.4 = (f32[3,53,53]{2,1,0:T(8,128)S(1)}, f32[3,53,53]{2,1,0:T(8,128)}, u32[]{:S(2)}) copy-start(f32[3,53,53]{2,1,0:T(8,128)} %implicit.1) | copy-start | bytes 101128
  0.7 12.2 %copy-start.3 = (f32[3,53,53]{2,1,0:T(8,128)S(1)}, f32[3,53,53]{2,1,0:T(8,128)}, u32[]{:S(2)}) copy-start(f32[3,53,53]{2,1,0:T(8,128)} %rate.3) | copy-start | bytes 101128
  0.7 12.2 %copy-start.5 = (s32[8192]{0:T(1024)S(1)}, s32[8192]{0:T(1024)}, u32[]{:S(2)}) copy-start(s32[8192]{0:T(1024)} %param.11) | copy-start | bytes 98308
  12.9 0.9 %copy-start.1 = (f32[9,56,128]{2,1,0:T(8,128)S(1)}, f32[9,56,128]{2,1,0:T(8,128)}, u32[]{:S(2)}) copy-start(f32[9,56,128]{2,1,0:T(8,128)} %shard_map.95.table) | copy-start | bytes 774148
